TPU v7x, 128 devices: a whole 4x4x4 slice. The times are simulated.
128 devices in a mesh: row: 8 (over x, core), col: 16 (over z, y).
Axes of the slice: x: 4, y: 4, z: 4, core: 2. Of those that a mesh axis runs over, the one named last changes fastest.
Arguments:
- moment_x: float32 [496, 496], P('row', 'col'), may hold values from -8 to 8
- zinv: float32 [496, 496], P('row', 'col'), may hold values from -8 to 8
- positions: int32 [4096, 16], P(('row', 'col')), may hold values from 0 to 495
- entry_count: int32 [4096], P(('row', 'col')), may hold values from 1 to 8
Outputs:
- schur: float32 [4096, 4096], P('row', 'col')
All inputs are finite; a program needn't handle non-finite values.
Results may differ from a plain program's by a relative error of at most 0.0003.
Values sent between devices are 32-bit elements; how exact they have to be, the bound alone decides.
A program may use at most 64 MiB of HBM per device.

v0:
```python
import jax
import jax.numpy as jnp
from jax import lax
from jax.sharding import PartitionSpec as P


def rows_first(arrays, axis, dims):
    turned = [jnp.moveaxis(a, dim, 0) for a, dim in zip(arrays, dims)]
    widths = [t[0].size for t in turned]
    both = jnp.concatenate([t.reshape(-1, w) for t, w in zip(turned, widths)], axis=1)
    out = lax.all_gather(both, axis, axis=0, tiled=True)
    blocks = jnp.split(out, [sum(widths[:k]) for k in range(1, len(widths))], axis=1)
    return tuple(
        (
            jnp.moveaxis(b.reshape(-1, *t.shape[1:]), 0, dim)
            for b, t, dim in zip(blocks, turned, dims)
        )
    )


def laid_out(blocks, dim):
    shape = list(blocks.shape[1:])
    shape[dim] *= blocks.shape[0]
    return jnp.moveaxis(blocks, 0, dim).reshape(shape)


def copy_for_each(value, axis):
    copies = jnp.broadcast_to(value, (lax.axis_size(axis), *value.shape))
    return lax.all_to_all(copies, axis, split_axis=0, concat_axis=0, tiled=True)


def gather_directly(value, axis, dim):
    return laid_out(copy_for_each(value, axis), dim)


def side_by_side(arrays, axis, dim, along):
    widths = [a.shape[along] for a in arrays]
    both = jnp.concatenate(arrays, axis=along)
    out = gather_directly(both, axis, dim)
    return tuple(jnp.split(out, [sum(widths[:k]) for k in range(1, len(widths))], axis=along))


def side_by_side_2(arrays, axis, dim, along):
    columns = [a.reshape(*a.shape[:along], -1) for a in arrays]
    both = jnp.concatenate(columns, axis=along)
    out, at, gathered = (lax.all_gather(both, axis, axis=dim, tiled=True), 0, [])
    for a, column in zip(arrays, columns):
        share = out[..., at : at + column.shape[along]]
        gathered.append(share.reshape(*share.shape[:along], *a.shape[along:]))
        at += column.shape[along]
    return tuple(gathered)


def picked(value, axis, root):
    return lax.dynamic_index_in_dim(lax.all_gather(value, axis), root, 0, keepdims=False)


def schur_rows(moment_x, zinv, row_positions, row_counts, col_positions, col_counts, group_rows):
    slot_count = row_positions.shape[1] // 2
    order_size = moment_x.shape[0]
    slot_iota = jnp.arange(slot_count, dtype=jnp.int32)
    whole_iota = jnp.arange(order_size, dtype=jnp.int32)
    col_left = col_positions[:, :slot_count].T.reshape(-1)
    col_right = col_positions[:, slot_count:].T.reshape(-1)
    col_alive = (slot_iota[:, None] < col_counts[None, :]).astype(jnp.float32).reshape(-1)
    pick_left = jnp.where(whole_iota[:, None] == col_left[None, :], col_alive[None, :], 0.0)
    pick_right = (whole_iota[:, None] == col_right[None, :]).astype(jnp.float32)
    ncols = col_positions.shape[0]
    nrows = row_positions.shape[0]

    def one_group(packed):
        grp_positions, grp_counts = packed
        grp_left = grp_positions[:, :slot_count].reshape(-1)
        grp_right = grp_positions[:, slot_count:].reshape(-1)
        grp_alive = (slot_iota[None, :] < grp_counts[:, None]).astype(jnp.float32).reshape(-1)
        x_rows = jnp.take(moment_x, grp_right, axis=0)
        w_rows = jnp.take(zinv, grp_left, axis=0)
        x_picked = jnp.dot(
            x_rows, pick_left, preferred_element_type=jnp.float32, precision=lax.Precision.HIGHEST
        )
        w_picked = jnp.dot(
            w_rows, pick_right, preferred_element_type=jnp.float32, precision=lax.Precision.HIGHEST
        )
        terms = x_picked * w_picked * grp_alive[:, None]
        return jnp.sum(terms.reshape(group_rows, slot_count, slot_count, ncols), axis=(1, 2))

    grouped = (
        row_positions.reshape(nrows // group_rows, group_rows, 2 * slot_count),
        row_counts.reshape(nrows // group_rows, group_rows),
    )
    return lax.map(one_group, grouped).reshape(nrows, ncols)


def collect(pieces):
    wide = rows_first((pieces[0], pieces[1]), "col", (1, 1))
    return side_by_side((wide[0], wide[1]), "row", 0, 1)


def shards(moment_x, zinv, positions, entry_count):
    full_x, full_w = collect((moment_x, zinv))
    row_positions, row_counts = side_by_side_2((positions, entry_count), "col", 0, 1)
    col_devices = lax.axis_size("col")
    share_ratio = col_devices // lax.axis_size("row")
    col_index = lax.axis_index("col")
    piece_size = row_counts.shape[0] // share_ratio
    offset_rows = col_index % share_ratio * piece_size
    piece_positions = lax.dynamic_slice_in_dim(row_positions, offset_rows, piece_size, 0)
    piece_counts = lax.dynamic_slice_in_dim(row_counts, offset_rows, piece_size, 0)
    col_positions, col_counts = (
        picked(piece_positions, "row", col_index // share_ratio),
        picked(piece_counts, "row", col_index // share_ratio),
    )
    group_rows = min(64, row_counts.shape[0])
    return schur_rows(
        full_x, full_w, row_positions, row_counts, col_positions, col_counts, group_rows
    )


def solution(mesh):
    return jax.shard_map(
        shards,
        mesh=mesh,
        in_specs=(P("row", "col"), P("row", "col"), P(("row", "col"), None), P(("row", "col"))),
        out_specs=P("row", "col"),
        check_vma=False,
    )
```

profile of v0, /device:TPU:1, one launch (start us, length us, event | category | flops | bytes accessed | tf_op | source)
XLA Modules:
  0.0 294.8 jit_solution(6078005898890789837)
XLA Ops:
  0.8 20.9 %all-gather.3 = f32[16,31,124]{2,1,0:T(8,128)S(1)} all-gather(f32[1,31,124]{2,1,0:T(8,128)S(1)} %maximum_bitcast_fusion), channel_id=1, replica_groups=mesh['row'=8,'col'=16] {'col'}, dimensions={0}, use_global_device_ids=true | all-gather | bytes 261392 | tf_op jit(solution)/shard_map/all_gather | solution.py:11
  23.7 10.2 %all-to-all-start = ((f32[8,62,992]{2,1,0:T(8,128)}), f32[8,62,992]{2,1,0:T(8,128)S(1)}, u32[]{:S(2)}, u32[]{:S(2)}) async-start(f32[8,62,992]{2,1,0:T(8,128)} %broadcast_in_dim.38), calls=%async_computation | async-start | bytes 4194304 | tf_op jit(solution)/shard_map/all_to_all | solution.py:29
  33.9 19.1 %all-gather.2 = s32[16,32,17]{1,2,0:T(8,128)S(1)} all-gather(s32[1,32,17]{1,2,0:T(8,128)S(1)} %add_bitcast_fusion), channel_id=1, replica_groups=mesh['row'=8,'col'=16] {'col'}, dimensions={0}, use_global_device_ids=true | all-gather | bytes 36992 | tf_op jit(solution)/shard_map/all_gather | solution.py:46
  53.4 17.6 %all-gather = s32[2048,16]{0,1:T(8,128)S(1)} all-gather(s32[256,16]{0,1:T(8,128)S(1)} %constant_dynamic-slice_fusion.4), channel_id=2, replica_groups=mesh['row'=8,'col'=16] {'row'}, dimensions={0}, use_global_device_ids=true | all-gather | bytes 147456 | tf_op jit(solution)/shard_map/all_gather | solution.py:55
  71.2 10.2 %all-gather.1 = s32[2048,1]{0,1:T(1,128)S(1)} all-gather(s32[256,1]{0,1:T(1,128)S(1)} %constant_dynamic-slice_fusion.2), channel_id=3, replica_groups=mesh['row'=8,'col'=16] {'row'}, dimensions={0}, use_global_device_ids=true | all-gather | bytes 9216 | tf_op jit(solution)/shard_map/all_gather | solution.py:55
  86.1 208.7 %while.11 = (s32[]{:T(128)}, f32[8,64,256]{2,1,0:T(8,128)}, s32[8,64,16]{2,1,0:T(8,128)S(1)}, f32[496,496]{1,0:T(8,128)S(1)}, f32[496,496]{1,0:T(8,128)S(1)}, /*...) while((s32[]{:T(128)}, f32[8,64,256]{2,1,0:T(8,128)}, ...), condition=%wide.region_2.4_spmd.clone, body=%wide.region_0.3_spmd.clone.sunk | while | flops 12489961472 | bytes 23157636 | solution.py:91
  88.0 8.6 %fusion.43 = f32[512,2048]{1,0:T(8,128)} fusion(f32[2048]{0:T(1024)S(1)} %get-tuple-element.213, s32[2048]{0:T(1024)S(1)} %get-tuple-element.212, f32[512,496]{1,0:T(8,128)S(1)} %gather_fusion, pred[512]{0:T(512)(128)(4,1)S(1)} %compare_and_fusion.4), kind=kOutput, calls=%fused_computation.9.clone.1 | convolution fusion | flops 6243409920 | bytes 5227008 | tf_op jit(solution)/shard_map/while/body/eval_jaxpr/dot_general | solution.py:78
  98.5 10.3 %multiply_multiply_fusion.2 = f32[512,2048]{1,0:T(8,128)} fusion(f32[512,2048]{1,0:T(8,128)} %fusion.43, f32[512]{0:T(512)S(1)} %reshape.133, s32[2048]{0:T(1024)S(1)} %get-tuple-element.214, f32[512,496]{1,0:T(8,128)S(1)} %gather_fusion.1, pred[512]{0:T(512)(128)(4,1)S(1)} %compare_and_fusion.5), kind=kOutput, calls=%fused_computation.5.clone.1 | convolution fusion | flops 6245507072 | bytes 9415168 | tf_op jit(solution)/shard_map/while/body/eval_jaxpr/dot_general | solution.py:81
  108.9 2.7 reduce_sum.11
  114.1 8.6 %fusion.43 = f32[512,2048]{1,0:T(8,128)} fusion(f32[2048]{0:T(1024)S(1)} %get-tuple-element.213, s32[2048]{0:T(1024)S(1)} %get-tuple-element.212, f32[512,496]{1,0:T(8,128)S(1)} %gather_fusion, pred[512]{0:T(512)(128)(4,1)S(1)} %compare_and_fusion.4), kind=kOutput, calls=%fused_computation.9.clone.1 | convolution fusion | flops 6243409920 | bytes 5227008 | tf_op jit(solution)/shard_map/while/body/eval_jaxpr/dot_general | solution.py:78
  124.6 10.3 %multiply_multiply_fusion.2 = f32[512,2048]{1,0:T(8,128)} fusion(f32[512,2048]{1,0:T(8,128)} %fusion.43, f32[512]{0:T(512)S(1)} %reshape.133, s32[2048]{0:T(1024)S(1)} %get-tuple-element.214, f32[512,496]{1,0:T(8,128)S(1)} %gather_fusion.1, pred[512]{0:T(512)(128)(4,1)S(1)} %compare_and_fusion.5), kind=kOutput, calls=%fused_computation.5.clone.1 | convolution fusion | flops 6245507072 | bytes 9415168 | tf_op jit(solution)/shard_map/while/body/eval_jaxpr/dot_general | solution.py:81
  140.1 8.6 %fusion.43 = f32[512,2048]{1,0:T(8,128)} fusion(f32[2048]{0:T(1024)S(1)} %get-tuple-element.213, s32[2048]{0:T(1024)S(1)} %get-tuple-element.212, f32[512,496]{1,0:T(8,128)S(1)} %gather_fusion, pred[512]{0:T(512)(128)(4,1)S(1)} %compare_and_fusion.4), kind=kOutput, calls=%fused_computation.9.clone.1 | convolution fusion | flops 6243409920 | bytes 5227008 | tf_op jit(solution)/shard_map/while/body/eval_jaxpr/dot_general | solution.py:78
  150.7 10.3 %multiply_multiply_fusion.2 = f32[512,2048]{1,0:T(8,128)} fusion(f32[512,2048]{1,0:T(8,128)} %fusion.43, f32[512]{0:T(512)S(1)} %reshape.133, s32[2048]{0:T(1024)S(1)} %get-tuple-element.214, f32[512,496]{1,0:T(8,128)S(1)} %gather_fusion.1, pred[512]{0:T(512)(128)(4,1)S(1)} %compare_and_fusion.5), kind=kOutput, calls=%fused_computation.5.clone.1 | convolution fusion | flops 6245507072 | bytes 9415168 | tf_op jit(solution)/shard_map/while/body/eval_jaxpr/dot_general | solution.py:81
  161.0 2.7 reduce_sum.11
  166.2 8.6 %fusion.43 = f32[512,2048]{1,0:T(8,128)} fusion(f32[2048]{0:T(1024)S(1)} %get-tuple-element.213, s32[2048]{0:T(1024)S(1)} %get-tuple-element.212, f32[512,496]{1,0:T(8,128)S(1)} %gather_fusion, pred[512]{0:T(512)(128)(4,1)S(1)} %compare_and_fusion.4), kind=kOutput, calls=%fused_computation.9.clone.1 | convolution fusion | flops 6243409920 | bytes 5227008 | tf_op jit(solution)/shard_map/while/body/eval_jaxpr/dot_general | solution.py:78
  176.8 10.3 %multiply_multiply_fusion.2 = f32[512,2048]{1,0:T(8,128)} fusion(f32[512,2048]{1,0:T(8,128)} %fusion.43, f32[512]{0:T(512)S(1)} %reshape.133, s32[2048]{0:T(1024)S(1)} %get-tuple-element.214, f32[512,496]{1,0:T(8,128)S(1)} %gather_fusion.1, pred[512]{0:T(512)(128)(4,1)S(1)} %compare_and_fusion.5), kind=kOutput, calls=%fused_computation.5.clone.1 | convolution fusion | flops 6245507072 | bytes 9415168 | tf_op jit(solution)/shard_map/while/body/eval_jaxpr/dot_general | solution.py:81
  192.3 8.6 %fusion.43 = f32[512,2048]{1,0:T(8,128)} fusion(f32[2048]{0:T(1024)S(1)} %get-tuple-element.213, s32[2048]{0:T(1024)S(1)} %get-tuple-element.212, f32[512,496]{1,0:T(8,128)S(1)} %gather_fusion, pred[512]{0:T(512)(128)(4,1)S(1)} %compare_and_fusion.4), kind=kOutput, calls=%fused_computation.9.clone.1 | convolution fusion | flops 6243409920 | bytes 5227008 | tf_op jit(solution)/shard_map/while/body/eval_jaxpr/dot_general | solution.py:78
  202.9 10.3 %multiply_multiply_fusion.2 = f32[512,2048]{1,0:T(8,128)} fusion(f32[512,2048]{1,0:T(8,128)} %fusion.43, f32[512]{0:T(512)S(1)} %reshape.133, s32[2048]{0:T(1024)S(1)} %get-tuple-element.214, f32[512,496]{1,0:T(8,128)S(1)} %gather_fusion.1, pred[512]{0:T(512)(128)(4,1)S(1)} %compare_and_fusion.5), kind=kOutput, calls=%fused_computation.5.clone.1 | convolution fusion | flops 6245507072 | bytes 9415168 | tf_op jit(solution)/shard_map/while/body/eval_jaxpr/dot_general | solution.py:81
  218.4 8.6 %fusion.43 = f32[512,2048]{1,0:T(8,128)} fusion(f32[2048]{0:T(1024)S(1)} %get-tuple-element.213, s32[2048]{0:T(1024)S(1)} %get-tuple-element.212, f32[512,496]{1,0:T(8,128)S(1)} %gather_fusion, pred[512]{0:T(512)(128)(4,1)S(1)} %compare_and_fusion.4), kind=kOutput, calls=%fused_computation.9.clone.1 | convolution fusion | flops 6243409920 | bytes 5227008 | tf_op jit(solution)/shard_map/while/body/eval_jaxpr/dot_general | solution.py:78
  229.0 10.3 %multiply_multiply_fusion.2 = f32[512,2048]{1,0:T(8,128)} fusion(f32[512,2048]{1,0:T(8,128)} %fusion.43, f32[512]{0:T(512)S(1)} %reshape.133, s32[2048]{0:T(1024)S(1)} %get-tuple-element.214, f32[512,496]{1,0:T(8,128)S(1)} %gather_fusion.1, pred[512]{0:T(512)(128)(4,1)S(1)} %compare_and_fusion.5), kind=kOutput, calls=%fused_computation.5.clone.1 | convolution fusion | flops 6245507072 | bytes 9415168 | tf_op jit(solution)/shard_map/while/body/eval_jaxpr/dot_general | solution.py:81
  244.5 8.6 %fusion.43 = f32[512,2048]{1,0:T(8,128)} fusion(f32[2048]{0:T(1024)S(1)} %get-tuple-element.213, s32[2048]{0:T(1024)S(1)} %get-tuple-element.212, f32[512,496]{1,0:T(8,128)S(1)} %gather_fusion, pred[512]{0:T(512)(128)(4,1)S(1)} %compare_and_fusion.4), kind=kOutput, calls=%fused_computation.9.clone.1 | convolution fusion | flops 6243409920 | bytes 5227008 | tf_op jit(solution)/shard_map/while/body/eval_jaxpr/dot_general | solution.py:78
  255.1 10.3 %multiply_multiply_fusion.2 = f32[512,2048]{1,0:T(8,128)} fusion(f32[512,2048]{1,0:T(8,128)} %fusion.43, f32[512]{0:T(512)S(1)} %reshape.133, s32[2048]{0:T(1024)S(1)} %get-tuple-element.214, f32[512,496]{1,0:T(8,128)S(1)} %gather_fusion.1, pred[512]{0:T(512)(128)(4,1)S(1)} %compare_and_fusion.5), kind=kOutput, calls=%fused_computation.5.clone.1 | convolution fusion | flops 6245507072 | bytes 9415168 | tf_op jit(solution)/shard_map/while/body/eval_jaxpr/dot_general | solution.py:81
  270.6 8.6 %fusion.43 = f32[512,2048]{1,0:T(8,128)} fusion(f32[2048]{0:T(1024)S(1)} %get-tuple-element.213, s32[2048]{0:T(1024)S(1)} %get-tuple-element.212, f32[512,496]{1,0:T(8,128)S(1)} %gather_fusion, pred[512]{0:T(512)(128)(4,1)S(1)} %compare_and_fusion.4), kind=kOutput, calls=%fused_computation.9.clone.1 | convolution fusion | flops 6243409920 | bytes 5227008 | tf_op jit(solution)/shard_map/while/body/eval_jaxpr/dot_general | solution.py:78
  281.1 10.3 %multiply_multiply_fusion.2 = f32[512,2048]{1,0:T(8,128)} fusion(f32[512,2048]{1,0:T(8,128)} %fusion.43, f32[512]{0:T(512)S(1)} %reshape.133, s32[2048]{0:T(1024)S(1)} %get-tuple-element.214, f32[512,496]{1,0:T(8,128)S(1)} %gather_fusion.1, pred[512]{0:T(512)(128)(4,1)S(1)} %compare_and_fusion.5), kind=kOutput, calls=%fused_computation.5.clone.1 | convolution fusion | flops 6245507072 | bytes 9415168 | tf_op jit(solution)/shard_map/while/body/eval_jaxpr/dot_general | solution.py:81
  (169 shorter events, 59.1 us)
Async XLA Ops:
  21.8 12.0 %copy-start = (s32[32,16]{0,1:T(8,128)S(1)}, s32[32,16]{0,1:T(8,128)}, u32[]{:S(2)}) copy-start(s32[32,16]{0,1:T(8,128)} %param.10) | copy-start | bytes 6148
  21.9 12.0 %copy-start.1 = (s32[32]{0:T(128)S(1)}, s32[32]{0:T(128)}, u32[]{:S(2)}) copy-start(s32[32]{0:T(128)} %param.11) | copy-start | bytes 388
  23.7 58.9 %all-to-all-start = ((f32[8,62,992]{2,1,0:T(8,128)}), f32[8,62,992]{2,1,0:T(8,128)S(1)}, u32[]{:S(2)}, u32[]{:S(2)}) async-start(f32[8,62,992]{2,1,0:T(8,128)} %broadcast_in_dim.38), calls=%async_computation | async-start | bytes 4194304 | tf_op jit(solution)/shard_map/all_to_all | solution.py:29
where the time goes:
time: 295 us
  matrix products  152 us (52%)
  blocking collectives  67.8 us (23%)
  local copies, waits for them, and re-layouts  40.4 us (14%)
  other arithmetic  24.2 us (8%)
  starting transfers between devices  10.2 us (3%)
    dot_general x8, matrix products, one_group(): jnp.dot(w_rows, pick_right, preferred_element_type=jnp.float32, precision...  82.6 us
    dot_general x8, matrix products, one_group(): jnp.dot(x_rows, pick_left, preferred_element_type=jnp.float32, precision=...  69 us
    all_gather x2, blocking collectives, picked(): lax.all_gather(value, axis)  27.8 us
    reduce_sum x8, other arithmetic, one_group(): jnp.sum(terms.reshape(group_rows, slot_count, slot_count, ncols), axis=(1...  21.8 us
    all_gather x1, blocking collectives, rows_first(): out = lax.all_gather(both, axis, axis=0, tiled=True)  20.9 us
    all_gather x1, blocking collectives, side_by_side_2(): lax.all_gather(both, axis, axis=dim, tiled=True)  19.1 us
    gather x8, local copies, waits for them, and re-layouts, one_group(): w_rows = jnp.take(zinv, grp_left, axis=0)  13 us
    gather x8, local copies, waits for them, and re-layouts, one_group(): x_rows = jnp.take(moment_x, grp_right, axis=0)  13 us
  transfers between devices with their start and end apart: 1, of which 0 were waited for; matrix products, arithmetic and copies ran while one was open for 1% of the time, Pallas kernels for 0%

commit v1 on v0

v1 whole, which is shorter than its diff:
```python
import functools

import jax
import jax.numpy as jnp
from jax import lax
from jax.experimental import pallas as pl
from jax.experimental.pallas import tpu as pltpu
from jax.sharding import PartitionSpec as P

MESH = pl.DeviceIdType.MESH
F32 = jnp.float32
BF16 = jnp.bfloat16
I32 = jnp.int32


def padded(v):
    return v + lax.shift_right_logical(v * 2115, 16)


def gather_kernel(x_ref, w_ref, pos_ref, cnt_ref, g_ref, gi_ref, slab, islab, send, recv, isend, irecv, psend, precv, loc):
    r = lax.axis_index("row")
    c = lax.axis_index("col")
    xx = r // 2
    core = r % 2
    zz = c // 4
    yy = c % 4
    me = 16 * r + c

    def peer(n):
        dx, dz, dy = n // 16, (n // 4) % 4, n % 4
        return (2 * ((xx + dx) % 4) + core, 4 * ((zz + dz) % 4) + (yy + dy) % 4)

    barrier = pltpu.get_barrier_semaphore()

    def greet(n, carry):
        pl.semaphore_signal(barrier, inc=1, device_id=peer(n), device_id_type=MESH)
        return carry

    lax.fori_loop(1, 64, greet, 0)
    partner = (r + 1 - 2 * core, c)
    pl.semaphore_signal(barrier, inc=1, device_id=partner, device_id_type=MESH)

    slab[...] = jnp.zeros_like(slab)
    slab[0:31, 0:31] = x_ref[0:31, :]
    slab[0:31, 32:63] = x_ref[31:62, :]
    slab[0:31, 64:95] = w_ref[0:31, :]
    slab[0:31, 96:127] = w_ref[31:62, :]

    post = jnp.transpose(pos_ref[...])
    slot = lax.broadcasted_iota(I32, (16, 32), 0) % 8
    live = slot < cnt_ref[...].reshape(1, 32)
    post = jnp.where(live, padded(post), 31)
    rows = jnp.transpose(post) * 8
    islab[...] = jnp.zeros_like(islab)
    for u in range(4):
        islab[:, 16 * u : 16 * u + 16] = rows[8 * u : 8 * u + 8, :]
    islab[:, 64:96] = post[0:8, :]
    islab[:, 96:128] = post[8:16, :]

    own = pltpu.make_async_copy(slab, g_ref.at[me], loc.at[0])
    iown = pltpu.make_async_copy(islab, gi_ref.at[me], loc.at[1])
    own.start()
    iown.start()
    pl.semaphore_wait(barrier, 64)

    def send_one(n, carry):
        to = peer(n)
        dx = n // 16
        pltpu.make_async_remote_copy(
            islab, gi_ref.at[me], isend, irecv.at[dx], device_id=to, device_id_type=MESH
        ).start()
        pltpu.make_async_remote_copy(
            slab, g_ref.at[me], send, recv.at[dx], device_id=to, device_id_type=MESH
        ).start()
        return carry

    lax.fori_loop(1, 64, send_one, 0)
    own.wait()
    iown.wait()

    for d in range(4):
        count = 15 if d == 0 else 16
        pltpu.make_async_copy(g_ref.at[0:count], g_ref.at[0:count], recv.at[d]).wait()
        pltpu.make_async_copy(gi_ref.at[0:count], gi_ref.at[0:count], irecv.at[d]).wait()
        src = 16 * (2 * ((xx + 4 - d) % 4) + core)
        pltpu.make_async_remote_copy(
            g_ref.at[pl.ds(src, 16)], g_ref.at[pl.ds(src, 16)], psend.at[0], precv.at[0],
            device_id=partner, device_id_type=MESH,
        ).start()
        pltpu.make_async_remote_copy(
            gi_ref.at[pl.ds(src, 16)], gi_ref.at[pl.ds(src, 16)], psend.at[1], precv.at[1],
            device_id=partner, device_id_type=MESH,
        ).start()
    pltpu.make_async_copy(g_ref.at[0:63], g_ref.at[0:63], send).wait()
    pltpu.make_async_copy(gi_ref.at[0:63], gi_ref.at[0:63], isend).wait()
    for sems in (psend, precv):
        pltpu.make_async_copy(g_ref.at[0:64], g_ref.at[0:64], sems.at[0]).wait()
        pltpu.make_async_copy(gi_ref.at[0:64], gi_ref.at[0:64], sems.at[1]).wait()


def table_kernel(g_ref, gi_ref, out_ref, sm, ci, xh, wh, tx0, tx1, tw0, tw1, pq, sem):
    r = lax.axis_index("row")
    c = lax.axis_index("col")
    rows_in = pltpu.make_async_copy(gi_ref.at[pl.ds(16 * r, 16)], sm, sem.at[0])
    rows_in.start()
    cols_in = pltpu.make_async_copy(gi_ref.at[pl.ds(8 * c, 8)], ci, sem.at[1])
    cols_in.start()

    lane = lax.broadcasted_iota(I32, (32, 128), 1)

    def assemble(rr, carry):
        for z in range(4):
            parts = [g_ref[16 * rr + 4 * z + y] for y in range(4)]
            for g in range(4):
                full = None
                for y in range(4):
                    turned = parts[y] if y == g else pltpu.roll(parts[y], (32 * (y - g)) % 128, 1)
                    full = turned if full is None else jnp.where(lane >= 32 * y, turned, full)
                hi = full.astype(BF16)
                lo = (full - hi.astype(F32)).astype(BF16)
                to = xh if g < 2 else wh
                at = pl.ds(pl.multiple_of(64 * rr + 32 * (g % 2), 32), 32)
                to[at, 128 * z : 128 * z + 128] = hi
                to[at, 512 + 128 * z : 640 + 128 * z] = lo
        return carry

    lax.fori_loop(0, 8, assemble, 0)
    cols_in.wait()
    lane8 = lax.broadcasted_iota(I32, (8, 128), 1)
    for half in range(2):
        for which in range(2):
            full = None
            for y in range(4):
                t = pltpu.roll(ci[4 * half + y], (32 * (y - 2 - which)) % 128, 1)
                full = t if full is None else jnp.where(lane8 >= 32 * y, t, full)
            pq[8 * which : 8 * which + 8, 128 * half : 128 * half + 128] = full

    place = lax.broadcasted_iota(I32, (512, 256), 0)

    def tables(l, carry):
        for which, half_ref, t0, t1 in ((0, xh, tx0, tx1), (1, wh, tw0, tw1)):
            picked = pq[pl.ds(8 * which + l, 1), :]
            hot = jnp.where(place == picked, 1.0, 0.0).astype(BF16)
            t = jnp.dot(half_ref[:, 0:512], hot, preferred_element_type=F32)
            t = t + jnp.dot(half_ref[:, 512:1024], hot, preferred_element_type=F32)
            t0[pl.ds(l, 512, stride=8), :] = t[:, 0:128]
            t1[pl.ds(l, 512, stride=8), :] = t[:, 128:256]
        return carry

    lax.fori_loop(0, 8, tables, 0)
    rows_in.wait()

    sub = lax.broadcasted_iota(I32, (8, 128), 0)
    low4, low2, low1 = sub < 4, sub % 4 < 2, sub % 2 < 1

    def folded(a):
        b = [
            jnp.where(low4, a[v], a[v + 4]) + pltpu.roll(jnp.where(low4, a[v + 4], a[v]), 4, 0)
            for v in range(4)
        ]
        d = [
            jnp.where(low2, b[v], pltpu.roll(b[v + 2], 2, 0))
            + jnp.where(low2, pltpu.roll(b[v], 6, 0), b[v + 2])
            for v in range(2)
        ]
        return jnp.where(low1, d[0], pltpu.roll(d[1], 1, 0)) + jnp.where(
            low1, pltpu.roll(d[0], 7, 0), d[1]
        )

    def group(n, carry):
        m, u = n // 4, n % 4
        left, right = [], []
        for v in range(8):
            a0, a1 = None, None
            for k in range(8):
                p = pl.multiple_of(sm[m, v, 16 * u + k], 8)
                q = pl.multiple_of(sm[m, v, 16 * u + 8 + k], 8)
                s0 = tx0[pl.ds(q, 8), :] * tw0[pl.ds(p, 8), :]
                s1 = tx1[pl.ds(q, 8), :] * tw1[pl.ds(p, 8), :]
                a0 = s0 if a0 is None else a0 + s0
                a1 = s1 if a1 is None else a1 + s1
            left.append(a0)
            right.append(a1)
        at = pl.ds(pl.multiple_of(8 * n, 8), 8)
        out_ref[at, 0:128] = folded(left)
        out_ref[at, 128:256] = folded(right)
        return carry

    lax.fori_loop(0, 64, group, 0)


def gather(x, w, pos, cnt):
    dma = pltpu.SemaphoreType.DMA
    return pl.pallas_call(
        gather_kernel,
        out_shape=(
            jax.ShapeDtypeStruct((128, 32, 128), F32),
            jax.ShapeDtypeStruct((128, 8, 128), I32),
        ),
        in_specs=[pl.BlockSpec(memory_space=pltpu.VMEM)] * 4,
        out_specs=(pl.BlockSpec(memory_space=pl.ANY), pl.BlockSpec(memory_space=pl.ANY)),
        scratch_shapes=[
            pltpu.VMEM((32, 128), F32),
            pltpu.VMEM((8, 128), I32),
            dma,
            dma((4,)),
            dma,
            dma((4,)),
            dma((2,)),
            dma((2,)),
            dma((2,)),
        ],
        compiler_params=pltpu.CompilerParams(collective_id=0, has_side_effects=True),
        name="gather",
    )(x, w, pos, cnt)


def tabled(g, gi):
    table = pltpu.VMEM((4096, 128), F32)
    return pl.pallas_call(
        table_kernel,
        out_shape=jax.ShapeDtypeStruct((512, 256), F32),
        in_specs=[pl.BlockSpec(memory_space=pltpu.VMEM), pl.BlockSpec(memory_space=pl.ANY)],
        out_specs=pl.BlockSpec(memory_space=pltpu.VMEM),
        scratch_shapes=[
            pltpu.SMEM((16, 8, 128), I32),
            pltpu.VMEM((8, 8, 128), I32),
            pltpu.VMEM((512, 1024), BF16),
            pltpu.VMEM((512, 1024), BF16),
            table,
            table,
            table,
            table,
            pltpu.VMEM((16, 256), I32),
            pltpu.SemaphoreType.DMA((2,)),
        ],
        compiler_params=pltpu.CompilerParams(vmem_limit_bytes=48 << 20),
        name="tables",
    )(g, gi)


def shards(moment_x, zinv, positions, entry_count):
    g, gi = gather(moment_x, zinv, positions, entry_count)
    return tabled(g, gi)


def solution(mesh):
    return jax.shard_map(
        shards,
        mesh=mesh,
        in_specs=(P("row", "col"), P("row", "col"), P(("row", "col"), None), P(("row", "col"))),
        out_specs=P("row", "col"),
        check_vma=False,
    )
```

time: 295 us -> 81 us (0.27)
  matrix products: 152 us -> 0 us
  Pallas kernels: 0 us -> 73.7 us
  blocking collectives: 67.8 us -> 0 us
  local copies, waits for them, and re-layouts: 40.4 us -> 6.82 us
  other arithmetic: 24.2 us -> 0 us
  starting transfers between devices: 10.2 us -> 0 us
    dot_general x16 -> x0, matrix products: 152 us -> none  [the longest x8 82.6 us: one_group(): jnp.dot(w_rows, pick_right, preferred_element_type=jnp.float32, precision...]
    pallas_call x0 -> x2, Pallas kernels: none -> 73.7 us  [the longest x1 39.8 us: tabled(): pl.pallas_call(table_kernel, out_shape=jax.ShapeDtypeStruct((512, 256), F...]
    all_gather x4 -> x0, blocking collectives: 67.8 us -> none  [the longest x2 27.8 us: picked(): lax.all_gather(value, axis)]
    gather x16 -> x0, local copies, waits for them, and re-layouts: 25.9 us -> none  [the longest x8 13 us: one_group(): w_rows = jnp.take(zinv, grp_left, axis=0)]
    reduce_sum x8 -> x0, other arithmetic: 21.8 us -> none  [one_group(): jnp.sum(terms.reshape(group_rows, slot_count, slot_count, ncols), axis=(1...]
    all_to_all x1 -> x0, starting transfers between devices: 10.2 us -> none  [copy_for_each(): return lax.all_to_all(copies, axis, split_axis=0, concat_axis=0, tiled=True)]
    unnamed x13 -> x7, local copies, waits for them, and re-layouts: 0.33 us -> 6.82 us
    dynamic_update_slice x8 -> x0, local copies, waits for them, and re-layouts: 5.12 us -> none  [schur_rows(): return lax.map(one_group, grouped).reshape(nrows, ncols)]
  transfers between devices with their start and end apart: 1 -> 0, of which waited for: 0 -> 0; matrix products, arithmetic and copies ran while one was open for 1% -> 0% of each run, Pallas kernels for 0% -> 0%
where the time goes in v1:
time: 81 us; the launch traced here: 80.6 us
  Pallas kernels  73.7 us (91%)
  local copies, waits for them, and re-layouts  6.82 us (8%)
    pallas_call x1, Pallas kernels, tabled(): pl.pallas_call(table_kernel, out_shape=jax.ShapeDtypeStruct((512, 256), F...  39.8 us
    pallas_call x1, Pallas kernels, gather(): pl.pallas_call(gather_kernel, out_shape=(jax.ShapeDtypeStruct((128, 32, 1...  34 us
    unnamed x7, local copies, waits for them, and re-layouts  6.82 us

profile of v1, /device:TPU:1, one launch (start us, length us, event | category | flops | bytes accessed | tf_op | source)
XLA Modules:
  0.0 80.6 jit_solution(8596863773588523710)
XLA Ops:
  0.0 1.4 %copy.7.pos_ref = s32[32,16]{1,0:T(8,128)} copy(s32[32,16]{0,1:T(8,128)} %param.6) | data formatting | bytes 4096 | tf_op args[2]
  1.4 1.4 %copy.5.x_ref = f32[62,31]{1,0:T(8,128)} copy(f32[62,31]{0,1:T(8,128)} %param.4) | data formatting | bytes 15376 | tf_op args[0]
  2.8 1.4 %copy.6.w_ref = f32[62,31]{1,0:T(8,128)} copy(f32[62,31]{0,1:T(8,128)} %param.5) | data formatting | bytes 15376 | tf_op args[1]
  4.2 34.0 %gather.1 = (f32[128,32,128]{2,1,0:T(8,128)}, s32[128,8,128]{2,1,0:T(8,128)}) custom-call(f32[62,31]{1,0:T(8,128)} %copy.5.x_ref, f32[62,31]{1,0:T(8,128)} %copy.6.w_ref, s32[32,16]{1,0:T(8,128)} %copy.7.pos_ref, s32[32]{0:T(128)} %cnt_ref.1), custom_call_target="tpu_custom_call" | custom-call | tf_op jit(solution)/shard_map/gather/pallas_call | solution.py:194
  38.2 0.0 copy-start
  38.2 1.6 %copy-done = f32[128,32,128]{2,1,0:T(8,128)S(1)} copy-done((f32[128,32,128]{2,1,0:T(8,128)S(1)}, f32[128,32,128]{2,1,0:T(8,128)}, u32[]{:S(2)}) %copy-start) | copy-done | bytes 2097176
  39.8 0.0 copy-start.1
  39.8 1.0 %copy-done.1 = s32[128,8,128]{2,1,0:T(8,128)S(1)} copy-done((s32[128,8,128]{2,1,0:T(8,128)S(1)}, s32[128,8,128]{2,1,0:T(8,128)}, u32[]{:S(2)}) %copy-start.1) | copy-done | bytes 524312
  40.8 39.8 %tables.1 = f32[512,256]{1,0:T(8,128)} custom-call(f32[128,32,128]{2,1,0:T(8,128)S(1)} %copy-done, s32[128,8,128]{2,1,0:T(8,128)S(1)} %copy-done.1), custom_call_target="tpu_custom_call" | custom-call | tf_op jit(solution)/shard_map/tables/pallas_call | solution.py:220
Async XLA Ops:
  38.2 1.6 %copy-start = (f32[128,32,128]{2,1,0:T(8,128)S(1)}, f32[128,32,128]{2,1,0:T(8,128)}, u32[]{:S(2)}) copy-start(f32[128,32,128]{2,1,0:T(8,128)} %get-tuple-element.7.g_ref) | copy-start | bytes 6291460
  39.8 1.0 %copy-start.1 = (s32[128,8,128]{2,1,0:T(8,128)S(1)}, s32[128,8,128]{2,1,0:T(8,128)}, u32[]{:S(2)}) copy-start(s32[128,8,128]{2,1,0:T(8,128)} %get-tuple-element.8.gi_ref) | copy-start | bytes 1572868

commit v2 on v1

v2 whole, which is shorter than its diff:
```python
import functools

import jax
import jax.numpy as jnp
from jax import lax
from jax.experimental import pallas as pl
from jax.experimental.pallas import tpu as pltpu
from jax.sharding import PartitionSpec as P

MESH = pl.DeviceIdType.MESH
F32 = jnp.float32
BF16 = jnp.bfloat16
I32 = jnp.int32


def padded(v, part, factor, pad):
    return v + pad * lax.shift_right_logical(v * factor, 16)


def gather_kernel(
    x_in, w_in, pos_in, cnt_in, ga, gb, gc,
    x_ref, w_ref, pos_ref, cnt_ref, slab_a, slab_b, slab_c, loc, s1, s2, s3, sp, r1, r2, r3, rp,
):
    r = lax.axis_index("row")
    c = lax.axis_index("col")
    core = r % 2
    here = (r // 2, c // 4, c % 4)
    ins = [
        pltpu.make_async_copy(a, b, loc.at[n])
        for n, (a, b) in enumerate(((x_in, x_ref), (w_in, w_ref), (pos_in, pos_ref), (cnt_in, cnt_ref)))
    ]
    for copy in ins:
        copy.start()

    def moved(axis, offset):
        at = list(here)
        at[axis] = (at[axis] + offset) % 4
        return at

    def device(at):
        return (2 * at[0] + core, 4 * at[1] + at[2])

    partner = (r + 1 - 2 * core, c)
    barrier = pltpu.get_barrier_semaphore()
    for axis in range(3):
        for offset in (1, 3, 2):
            pl.semaphore_signal(barrier, inc=1, device_id=device(moved(axis, offset)), device_id_type=MESH)
    pl.semaphore_signal(barrier, inc=1, device_id=partner, device_id_type=MESH)

    for ref in (slab_a, slab_b, slab_c):
        ref[...] = jnp.zeros_like(ref)
    for copy in ins:
        copy.wait()
    for lanes, src in ((0, x_ref), (64, w_ref)):
        slab_a[:, lanes : lanes + 62] = src[0:16, :]
        slab_b[0:8, lanes : lanes + 62] = src[16:24, :]
        slab_c[0:7, lanes : lanes + 62] = src[24:31, :]

    pos = pos_ref[...]
    live = lax.broadcasted_iota(I32, (16, 32), 0) % 8 < cnt_ref[...].reshape(1, 32)
    cols = jnp.where(live, padded(pos, 62, 1058, 2), 62).astype(F32)
    rows = jnp.where(live, padded(pos, 31, 2115, 1), 31).astype(F32) * 8.0
    rows = jnp.transpose(rows)
    for u in range(4):
        slab_b[8:16, 16 * u : 16 * u + 16] = rows[8 * u : 8 * u + 8, :]
    slab_b[8:16, 64:96] = cols[0:8, :]
    slab_b[8:16, 96:128] = cols[8:16, :]

    every = pl.ds(0, 4)
    parts = ((ga, slab_a, (0, 2, 1)), (gb, slab_b, (2, 1, 0)), (gc, slab_c, (1, 0, 2)))

    def box(g, at, open_axes=()):
        index = [every if axis in open_axes else at[axis] for axis in range(3)]
        return g.at[index[0], core, index[1], index[2]]

    own = [
        pltpu.make_async_copy(slab, box(g, here), loc.at[4 + n]) for n, (g, slab, order) in enumerate(parts)
    ]
    for copy in own:
        copy.start()
    pl.semaphore_wait(barrier, 10)

    def send(src, dst, send_sem, recv_sem, to):
        pltpu.make_async_remote_copy(
            src, dst, send_sem, recv_sem, device_id=to, device_id_type=MESH
        ).start()

    def wait(ref, sem):
        pltpu.make_async_copy(ref, ref, sem).wait()

    for n, (g, slab, order) in enumerate(parts):
        for offset in (1, 3, 2):
            send(slab, box(g, here), s1.at[n], r1.at[n], device(moved(order[0], offset)))
    for copy in own:
        copy.wait()
    for n, (g, slab, order) in enumerate(parts):
        wait(g.at[0, 0, 0, 0:3], r1.at[n])
        line = box(g, here, order[:1])
        for offset in (1, 3, 2):
            send(line, line, s2.at[n], r2.at[n, offset - 1], device(moved(order[1], offset)))
        for offset in (1, 3, 2):
            send(line, line, s3.at[n], r3.at[n, offset - 1], device(moved(order[2], offset)))
    for back in (1, 3, 2):
        for n, (g, slab, order) in enumerate(parts):
            wait(g.at[0, 0, 0, 0:4], r2.at[n, back - 1])
            line = box(g, moved(order[1], 4 - back), order[:1])
            for offset in (1, 3, 2):
                send(line, line, s3.at[n], r3.at[n, offset - 1], device(moved(order[2], offset)))
    for n, (g, slab, order) in enumerate(parts):
        plane = box(g, here, order[:2])
        send(plane, plane, sp.at[n], rp.at[n], partner)
    for back in (1, 3, 2):
        for n, (g, slab, order) in enumerate(parts):
            wait(g.at[0, 0], r3.at[n, back - 1])
            plane = box(g, moved(order[2], 4 - back), order[:2])
            send(plane, plane, sp.at[n], rp.at[n], partner)
    for n, (g, slab, order) in enumerate(parts):
        wait(g.at[0, 0, 0, 0:3], s1.at[n])
        wait(g.at[0, 0, 0:3], s2.at[n])
        wait(g.at[0:3, 0], s3.at[n])
        wait(g.at[:, 0], sp.at[n])
        wait(g.at[:, 0], rp.at[n])


def table_kernel(ga_ref, gb_ref, gc_ref, out_ref, sm, flat, xh, tx, pq, sem, acc):
    r = lax.axis_index("row")
    c = lax.axis_index("col")

    lane16 = lax.broadcasted_iota(I32, (16, 128), 1)
    by_row = [gb_ref[pl.ds(256 * r + 8 + v, 16, stride=16), :] for v in range(8)]
    for u in range(4):
        full = None
        for v in range(8):
            turn = (16 * (v - u)) % 128
            t = by_row[v] if turn == 0 else pltpu.roll(by_row[v], turn, 1)
            full = t if full is None else jnp.where(lane16 >= 16 * v, t, full)
        flat[pl.ds(u, 16, stride=4), :] = full.astype(I32)
    to_scalar = pltpu.make_async_copy(flat, sm, sem)
    to_scalar.start()

    lane8 = lax.broadcasted_iota(I32, (8, 128), 1)
    for half in range(2):
        for which in range(2):
            full = None
            for y in range(4):
                tile = gb_ref[pl.ds(pl.multiple_of(16 * (8 * c + 4 * half + y) + 8, 8), 8), :]
                turn = (32 * (y - 2 - which)) % 128
                t = tile if turn == 0 else pltpu.roll(tile, turn, 1)
                full = t if full is None else jnp.where(lane8 >= 32 * y, t, full)
            pq[8 * which : 8 * which + 8, 128 * half : 128 * half + 128] = full.astype(I32)

    left = lane16 < 64

    def assemble(cc, carry):
        for xx in range(4):
            even, odd = 32 * xx + cc, 32 * xx + 16 + cc
            tops = [ga_ref[pl.ds(pl.multiple_of(16 * d, 16), 16), :] for d in (even, odd)]
            lows = [
                jnp.concatenate(
                    [
                        gb_ref[pl.ds(pl.multiple_of(16 * d, 16), 8), :],
                        gc_ref[pl.ds(pl.multiple_of(8 * d, 8), 8), :],
                    ],
                    axis=0,
                )
                for d in (even, odd)
            ]
            for low, (a, b) in enumerate((tops, lows)):
                for which in range(2):
                    if which == 0:
                        full = jnp.where(left, a, pltpu.roll(b, 64, 1))
                    else:
                        full = jnp.where(left, pltpu.roll(a, 64, 1), b)
                    hi = full.astype(BF16)
                    lo = (full - hi.astype(F32)).astype(BF16)
                    at = pl.ds(pl.multiple_of(512 * which + 32 * cc + 16 * low, 16), 16)
                    xh[at, 128 * xx : 128 * xx + 128] = hi
                    xh[at, 512 + 128 * xx : 640 + 128 * xx] = lo
        return carry

    lax.fori_loop(0, 16, assemble, 0)

    place = lax.broadcasted_iota(I32, (512, 256), 0)

    def tables(n, carry):
        which, l = n // 8, n % 8
        picked = pq[pl.ds(n, 1), :]
        hot = jnp.where(place == picked, 1.0, 0.0).astype(BF16)
        t = jnp.dot(
            xh[pl.ds(pl.multiple_of(512 * which, 512), 512), :],
            jnp.concatenate([hot, hot], axis=0),
            preferred_element_type=F32,
        )
        tx[pl.ds(8192 * which + l, 512, stride=8), :] = t[:, 0:128]
        tx[pl.ds(8192 * which + 4096 + l, 512, stride=8), :] = t[:, 128:256]
        return carry

    lax.fori_loop(0, 16, tables, 0)
    to_scalar.wait()

    sub = lax.broadcasted_iota(I32, (8, 128), 0)
    low4, low2, low1 = sub < 4, sub % 4 < 2, sub % 2 < 1

    def folded(a):
        b = [
            jnp.where(low4, a[v], a[v + 4]) + pltpu.roll(jnp.where(low4, a[v + 4], a[v]), 4, 0)
            for v in range(4)
        ]
        d = [
            jnp.where(low2, b[v], pltpu.roll(b[v + 2], 2, 0))
            + jnp.where(low2, pltpu.roll(b[v], 6, 0), b[v + 2])
            for v in range(2)
        ]
        return jnp.where(low1, d[0], pltpu.roll(d[1], 1, 0)) + jnp.where(
            low1, pltpu.roll(d[0], 7, 0), d[1]
        )

    def fold_group(n, slot):
        at = pl.ds(pl.multiple_of(8 * n, 8), 8)
        for half in range(2):
            here = [acc[pl.ds(pl.multiple_of(128 * slot + 64 * half + 8 * v, 8), 8), :] for v in range(8)]
            out_ref[at, 128 * half : 128 * half + 128] = folded(here)

    def group(n, carry):
        slot = n % 2
        fold_group(jnp.maximum(n - 1, 0), 1 - slot)
        for v in range(8):
            a0, a1 = None, None
            for k in range(8):
                p = pl.multiple_of(sm[n, 16 * v + k], 8)
                q = pl.multiple_of(sm[n, 16 * v + 8 + k], 8)
                s0 = tx[pl.ds(q, 8), :] * tx[pl.ds(p + 8192, 8), :]
                s1 = tx[pl.ds(q + 4096, 8), :] * tx[pl.ds(p + 12288, 8), :]
                a0 = s0 if a0 is None else a0 + s0
                a1 = s1 if a1 is None else a1 + s1
            acc[pl.ds(pl.multiple_of(128 * slot + 8 * v, 8), 8), :] = a0
            acc[pl.ds(pl.multiple_of(128 * slot + 64 + 8 * v, 8), 8), :] = a1
        return carry

    lax.fori_loop(0, 64, group, 0)
    fold_group(63, 1)


def gather(x, w, pos, cnt):
    dma = pltpu.SemaphoreType.DMA
    return pl.pallas_call(
        gather_kernel,
        out_shape=tuple(jax.ShapeDtypeStruct((4, 2, 4, 4, n, 128), F32) for n in (16, 16, 8)),
        in_specs=[pl.BlockSpec(memory_space=pl.ANY)] * 4,
        out_specs=tuple(pl.BlockSpec(memory_space=pl.ANY) for n in range(3)),
        scratch_shapes=[
            pltpu.VMEM((31, 62), F32),
            pltpu.VMEM((31, 62), F32),
            pltpu.VMEM((16, 32), I32),
            pltpu.VMEM((32,), I32),
            pltpu.VMEM((16, 128), F32),
            pltpu.VMEM((16, 128), F32),
            pltpu.VMEM((8, 128), F32),
            dma((7,)),
            dma((3,)),
            dma((3,)),
            dma((3,)),
            dma((3,)),
            dma((3,)),
            dma((3, 3)),
            dma((3, 3)),
            dma((3,)),
        ],
        compiler_params=pltpu.CompilerParams(collective_id=0, has_side_effects=True),
        name="gather",
    )(x, w, pos, cnt)


def tabled(ga, gb, gc):
    return pl.pallas_call(
        table_kernel,
        out_shape=jax.ShapeDtypeStruct((512, 256), F32),
        in_specs=[pl.BlockSpec(memory_space=pltpu.VMEM)] * 3,
        out_specs=pl.BlockSpec(memory_space=pltpu.VMEM),
        scratch_shapes=[
            pltpu.SMEM((64, 128), I32),
            pltpu.VMEM((64, 128), I32),
            pltpu.VMEM((1024, 1024), BF16),
            pltpu.VMEM((16384, 128), F32),
            pltpu.VMEM((16, 256), I32),
            pltpu.SemaphoreType.DMA,
            pltpu.VMEM((256, 128), F32),
        ],
        compiler_params=pltpu.CompilerParams(vmem_limit_bytes=48 << 20),
        name="tables",
    )(ga, gb, gc)


def shards(moment_x, zinv, positions, entry_count):
    g = gather(moment_x.T, zinv.T, positions.T, entry_count)
    return tabled(*(a.reshape(-1, 128) for a in g))


def solution(mesh):
    return jax.shard_map(
        shards,
        mesh=mesh,
        in_specs=(P("row", "col"), P("row", "col"), P(("row", "col"), None), P(("row", "col"))),
        out_specs=P("row", "col"),
        check_vma=False,
    )
```

time: 81 us -> 47.6 us (0.59)
  Pallas kernels: 73.7 us -> 43.8 us
  local copies, waits for them, and re-layouts: 6.82 us -> 3.48 us
    pallas_call x1, Pallas kernels: 39.8 us -> 19.6 us  [tabled(): pl.pallas_call(table_kernel, out_shape=jax.ShapeDtypeStruct((512, 256), F...]
    pallas_call x1, Pallas kernels: 34 us -> 24.2 us  [gather(): pl.pallas_call(gather_kernel, out_shape=tuple((jax.ShapeDtypeStruct((4, 2...]
    unnamed x7 -> x6, local copies, waits for them, and re-layouts: 6.82 us -> 3.48 us
where the time goes in v2:
time: 47.6 us; the launch traced here: 47.3 us
  Pallas kernels  43.8 us (92%)
  local copies, waits for them, and re-layouts  3.48 us (7%)
    pallas_call x1, Pallas kernels, gather(): pl.pallas_call(gather_kernel, out_shape=tuple((jax.ShapeDtypeStruct((4, 2...  24.2 us
    pallas_call x1, Pallas kernels, tabled(): pl.pallas_call(table_kernel, out_shape=jax.ShapeDtypeStruct((512, 256), F...  19.6 us
    unnamed x6, local copies, waits for them, and re-layouts  3.48 us

profile of v2, /device:TPU:1, one launch (start us, length us, event | category | flops | bytes accessed | tf_op | source)
XLA Modules:
  0.0 47.3 jit_solution(12660696093725285847)
XLA Ops:
  0.0 24.2 %gather.1 = (f32[4,2,4,4,16,128]{5,4,3,2,1,0:T(8,128)}, f32[4,2,4,4,16,128]{5,4,3,2,1,0:T(8,128)}, f32[4,2,4,4,8,128]{5,4,3,2,1,0:T(8,128)}) custom-call(f32[31,62]{1,0:T(8,128)} %bitcast.9, f32[31,62]{1,0:T(8,128)} %bitcast.10, s32[16,32]{1,0:T(8,128)} %bitcast.11, s32[32]{0:T(128)} %cnt_in.1), custom_call_target="tpu_custom_call" | custom-call | tf_op jit(solution)/shard_map/gather/pallas_call | solution.py:246
  24.2 0.0 copy-start
  24.2 1.2 %copy-done = f32[4,2,4,4,16,128]{5,4,3,2,1,0:T(8,128)S(1)} copy-done((f32[4,2,4,4,16,128]{5,4,3,2,1,0:T(8,128)S(1)}, f32[4,2,4,4,16,128]{5,4,3,2,1,0:T(8,128)}, u32[]{:S(2)}) %copy-start) | copy-done | bytes 1048600
  25.5 0.0 copy-start.1
  25.5 1.2 %copy-done.1 = f32[4,2,4,4,16,128]{5,4,3,2,1,0:T(8,128)S(1)} copy-done((f32[4,2,4,4,16,128]{5,4,3,2,1,0:T(8,128)S(1)}, f32[4,2,4,4,16,128]{5,4,3,2,1,0:T(8,128)}, u32[]{:S(2)}) %copy-start.1) | copy-done | bytes 1048600
  26.7 0.0 copy-start.2
  26.7 1.0 %copy-done.2 = f32[4,2,4,4,8,128]{5,4,3,2,1,0:T(8,128)S(1)} copy-done((f32[4,2,4,4,8,128]{5,4,3,2,1,0:T(8,128)S(1)}, f32[4,2,4,4,8,128]{5,4,3,2,1,0:T(8,128)}, u32[]{:S(2)}) %copy-start.2) | copy-done | bytes 524312
  27.7 19.6 %tables.1 = f32[512,256]{1,0:T(8,128)} custom-call(f32[2048,128]{1,0:T(8,128)S(1)} %bitcast.6, f32[2048,128]{1,0:T(8,128)S(1)} %bitcast.7, f32[1024,128]{1,0:T(8,128)S(1)} %bitcast.8), custom_call_target="tpu_custom_call" | custom-call | tf_op jit(solution)/shard_map/tables/pallas_call | solution.py:275
Async XLA Ops:
  24.2 1.2 %copy-start = (f32[4,2,4,4,16,128]{5,4,3,2,1,0:T(8,128)S(1)}, f32[4,2,4,4,16,128]{5,4,3,2,1,0:T(8,128)}, u32[]{:S(2)}) copy-start(f32[4,2,4,4,16,128]{5,4,3,2,1,0:T(8,128)} %get-tuple-element.8) | copy-start | bytes 3145732
  25.5 1.2 %copy-start.1 = (f32[4,2,4,4,16,128]{5,4,3,2,1,0:T(8,128)S(1)}, f32[4,2,4,4,16,128]{5,4,3,2,1,0:T(8,128)}, u32[]{:S(2)}) copy-start(f32[4,2,4,4,16,128]{5,4,3,2,1,0:T(8,128)} %get-tuple-element.9) | copy-start | bytes 3145732
  26.7 1.0 %copy-start.2 = (f32[4,2,4,4,8,128]{5,4,3,2,1,0:T(8,128)S(1)}, f32[4,2,4,4,8,128]{5,4,3,2,1,0:T(8,128)}, u32[]{:S(2)}) copy-start(f32[4,2,4,4,8,128]{5,4,3,2,1,0:T(8,128)} %get-tuple-element.10) | copy-start | bytes 1572868

commit v3 on v2

--- a/solution.py
+++ b/solution.py
@@ -59,7 +59,7 @@
     pos = pos_ref[...]
     live = lax.broadcasted_iota(I32, (16, 32), 0) % 8 < cnt_ref[...].reshape(1, 32)
     cols = jnp.where(live, padded(pos, 62, 1058, 2), 62).astype(F32)
-    rows = jnp.where(live, padded(pos, 31, 2115, 1), 31).astype(F32) * 8.0
+    rows = jnp.where(live, padded(pos, 31, 2115, 1), 31).astype(F32) * 16.0
     rows = jnp.transpose(rows)
     for u in range(4):
         slab_b[8:16, 16 * u : 16 * u + 16] = rows[8 * u : 8 * u + 8, :]
@@ -191,8 +191,8 @@
             jnp.concatenate([hot, hot], axis=0),
             preferred_element_type=F32,
         )
-        tx[pl.ds(8192 * which + l, 512, stride=8), :] = t[:, 0:128]
-        tx[pl.ds(8192 * which + 4096 + l, 512, stride=8), :] = t[:, 128:256]
+        tx[pl.ds(8192 * which + l, 512, stride=16), :] = t[:, 0:128]
+        tx[pl.ds(8192 * which + 8 + l, 512, stride=16), :] = t[:, 128:256]
         return carry
 
     lax.fori_loop(0, 16, tables, 0)
@@ -230,7 +230,7 @@
                 p = pl.multiple_of(sm[n, 16 * v + k], 8)
                 q = pl.multiple_of(sm[n, 16 * v + 8 + k], 8)
                 s0 = tx[pl.ds(q, 8), :] * tx[pl.ds(p + 8192, 8), :]
-                s1 = tx[pl.ds(q + 4096, 8), :] * tx[pl.ds(p + 12288, 8), :]
+                s1 = tx[pl.ds(q + 8, 8), :] * tx[pl.ds(p + 8200, 8), :]
                 a0 = s0 if a0 is None else a0 + s0
                 a1 = s1 if a1 is None else a1 + s1
             acc[pl.ds(pl.multiple_of(128 * slot + 8 * v, 8), 8), :] = a0
@@ -246,8 +246,8 @@
     return pl.pallas_call(
         gather_kernel,
         out_shape=tuple(jax.ShapeDtypeStruct((4, 2, 4, 4, n, 128), F32) for n in (16, 16, 8)),
-        in_specs=[pl.BlockSpec(memory_space=pl.ANY)] * 4,
-        out_specs=tuple(pl.BlockSpec(memory_space=pl.ANY) for n in range(3)),
+        in_specs=[pl.BlockSpec(memory_space=pltpu.HBM)] * 4,
+        out_specs=tuple(pl.BlockSpec(memory_space=pltpu.VMEM) for n in range(3)),
         scratch_shapes=[
             pltpu.VMEM((31, 62), F32),
             pltpu.VMEM((31, 62), F32),
@@ -266,7 +266,7 @@
             dma((3, 3)),
             dma((3,)),
         ],
-        compiler_params=pltpu.CompilerParams(collective_id=0, has_side_effects=True),
+        compiler_params=pltpu.CompilerParams(collective_id=0, has_side_effects=True, vmem_limit_bytes=8 << 20),
         name="gather",
     )(x, w, pos, cnt)
 
@@ -286,13 +286,13 @@
             pltpu.SemaphoreType.DMA,
             pltpu.VMEM((256, 128), F32),
         ],
-        compiler_params=pltpu.CompilerParams(vmem_limit_bytes=48 << 20),
+        compiler_params=pltpu.CompilerParams(vmem_limit_bytes=40 << 20),
         name="tables",
     )(ga, gb, gc)
 
 
 def shards(moment_x, zinv, positions, entry_count):
-    g = gather(moment_x.T, zinv.T, positions.T, entry_count)
+    g = gather(*(pltpu.with_memory_space_constraint(a, pltpu.HBM) for a in (moment_x.T, zinv.T, positions.T, entry_count)))
     return tabled(*(a.reshape(-1, 128) for a in g))
 
 

time: 47.6 us -> 41.5 us (0.87)
  local copies, waits for them, and re-layouts: 3.48 us -> 0 us
  Pallas kernels: 43.8 us -> 41.3 us
    unnamed x6 -> x0, local copies, waits for them, and re-layouts: 3.48 us -> none
    pallas_call x1, Pallas kernels: 24.2 us -> 23 us  [gather(): pl.pallas_call(gather_kernel, out_shape=tuple((jax.ShapeDtypeStruct((4, 2...]
    pallas_call x1, Pallas kernels: 19.6 us -> 18.3 us  [tabled(): pl.pallas_call(table_kernel, out_shape=jax.ShapeDtypeStruct((512, 256), F...]
where the time goes in v3:
time: 41.5 us; the launch traced here: 41.3 us
  Pallas kernels  41.3 us (100%)
    pallas_call x1, Pallas kernels, gather(): pl.pallas_call(gather_kernel, out_shape=tuple((jax.ShapeDtypeStruct((4, 2...  23 us
    pallas_call x1, Pallas kernels, tabled(): pl.pallas_call(table_kernel, out_shape=jax.ShapeDtypeStruct((512, 256), F...  18.3 us

profile of v3, /device:TPU:1, one launch (start us, length us, event | category | flops | bytes accessed | tf_op | source)
XLA Modules:
  0.0 41.3 jit_solution(192868198446066337)
XLA Ops:
  0.0 23.0 %gather.1 = (f32[4,2,4,4,16,128]{5,4,3,2,1,0:T(8,128)S(1)}, f32[4,2,4,4,16,128]{5,4,3,2,1,0:T(8,128)S(1)}, f32[4,2,4,4,8,128]{5,4,3,2,1,0:T(8,128)S(1)}) custom-call(f32[31,62]{1,0:T(8,128)} %bitcast.9, f32[31,62]{1,0:T(8,128)} %bitcast.10, s32[16,32]{1,0:T(8,128)} %bitcast.11, s32[32]{0:T(128)} %cnt_in.1), custom_call_target="tpu_custom_call" | custom-call | tf_op jit(solution)/shard_map/gather/pallas_call | solution.py:246
  23.0 18.3 %tables.1 = f32[512,256]{1,0:T(8,128)} custom-call(f32[2048,128]{1,0:T(8,128)S(1)} %bitcast.6, f32[2048,128]{1,0:T(8,128)S(1)} %bitcast.7, f32[1024,128]{1,0:T(8,128)S(1)} %bitcast.8), custom_call_target="tpu_custom_call" | custom-call | tf_op jit(solution)/shard_map/tables/pallas_call | solution.py:275

commit v4 on v3

v4 whole, which is shorter than its diff:
```python
import functools

import jax
import jax.numpy as jnp
from jax import lax
from jax.experimental import pallas as pl
from jax.experimental.pallas import tpu as pltpu
from jax.sharding import PartitionSpec as P

MESH = pl.DeviceIdType.MESH
F32 = jnp.float32
BF16 = jnp.bfloat16
I32 = jnp.int32


def padded(v, part, factor, pad):
    return v + pad * lax.shift_right_logical(v * factor, 16)


def gather_kernel(
    x_in, w_in, pos_in, cnt_in, gi, xh, hot,
    ga, gc, x_ref, w_ref, pos_ref, cnt_ref, slab_a, slab_c, slab_i, pq, loc, s1, s2, s3, sp, r1, r2, r3, rp,
):
    r = lax.axis_index("row")
    c = lax.axis_index("col")
    core = r % 2
    here = (r // 2, c // 4, c % 4)
    ins = [
        pltpu.make_async_copy(a, b, loc.at[n])
        for n, (a, b) in enumerate(((x_in, x_ref), (w_in, w_ref), (pos_in, pos_ref), (cnt_in, cnt_ref)))
    ]
    for copy in ins:
        copy.start()

    def moved(axis, offset):
        at = list(here)
        at[axis] = (at[axis] + offset) % 4
        return at

    def device(at):
        return (2 * at[0] + core, 4 * at[1] + at[2])

    partner = (r + 1 - 2 * core, c)
    barrier = pltpu.get_barrier_semaphore()
    for axis in range(3):
        for offset in (1, 3, 2):
            pl.semaphore_signal(barrier, inc=1, device_id=device(moved(axis, offset)), device_id_type=MESH)
    pl.semaphore_signal(barrier, inc=1, device_id=partner, device_id_type=MESH)

    for ref in (slab_a, slab_c, slab_i):
        ref[...] = jnp.zeros_like(ref)
    for copy in ins:
        copy.wait()
    for lanes, src in ((0, x_ref), (64, w_ref)):
        slab_a[:, lanes : lanes + 62] = src[0:16, :]
        slab_c[0:15, lanes : lanes + 62] = src[16:31, :]

    pos = pos_ref[...]
    live = lax.broadcasted_iota(I32, (16, 32), 0) % 8 < cnt_ref[...].reshape(1, 32)
    cols = jnp.where(live, padded(pos, 62, 1058, 2), 62).astype(F32)
    rows = jnp.where(live, padded(pos, 31, 2115, 1), 31).astype(F32) * 8.0
    rows = jnp.transpose(rows)
    for u in range(4):
        slab_i[:, 16 * u : 16 * u + 16] = rows[8 * u : 8 * u + 8, :]
    slab_i[:, 64:96] = cols[0:8, :]
    slab_i[:, 96:128] = cols[8:16, :]

    every = pl.ds(0, 4)
    parts = ((gi, slab_i, (2, 1, 0)), (ga, slab_a, (2, 0, 1)), (gc, slab_c, (1, 0, 2)))

    def box(g, at, open_axes=()):
        index = [every if axis in open_axes else at[axis] for axis in range(3)]
        return g.at[index[0], core, index[1], index[2]]

    own = [
        pltpu.make_async_copy(slab, box(g, here), loc.at[4 + n]) for n, (g, slab, order) in enumerate(parts)
    ]
    for copy in own:
        copy.start()
    pl.semaphore_wait(barrier, 10)

    def send(src, dst, send_sem, recv_sem, to):
        pltpu.make_async_remote_copy(
            src, dst, send_sem, recv_sem, device_id=to, device_id_type=MESH
        ).start()

    def wait(ref, sem):
        pltpu.make_async_copy(ref, ref, sem).wait()

    for n, (g, slab, order) in enumerate(parts):
        for offset in (1, 3, 2):
            send(slab, box(g, here), s1.at[n], r1.at[n], device(moved(order[0], offset)))
    for copy in own:
        copy.wait()
    for n, (g, slab, order) in enumerate(parts):
        wait(g.at[0, 0, 0, 0:3], r1.at[n])
        line = box(g, here, order[:1])
        for offset in (1, 3, 2):
            send(line, line, s2.at[n], r2.at[n, offset - 1], device(moved(order[1], offset)))
        for offset in (1, 3, 2):
            send(line, line, s3.at[n], r3.at[n, offset - 1], device(moved(order[2], offset)))
    for back in (1, 3, 2):
        for n, (g, slab, order) in enumerate(parts):
            wait(g.at[0, 0, 0, 0:4], r2.at[n, back - 1])
            line = box(g, moved(order[1], 4 - back), order[:1])
            for offset in (1, 3, 2):
                send(line, line, s3.at[n], r3.at[n, offset - 1], device(moved(order[2], offset)))
    left = lax.broadcasted_iota(I32, (16, 128), 1) < 64

    def split(g, plane, along_z, first):
        for step in range(4):
            z, y = (plane, step) if along_z else (step, plane)
            for xx in range(4):
                even, odd = g[xx, 0, z, y], g[xx, 1, z, y]
                both = (
                    jnp.where(left, even, pltpu.roll(odd, 64, 1)),
                    jnp.where(left, pltpu.roll(even, 64, 1), odd),
                )
                for which, full in enumerate(both):
                    hi = full.astype(BF16)
                    lo = (full - hi.astype(F32)).astype(BF16)
                    at = pl.ds(pl.multiple_of(512 * which + 32 * (4 * z + y) + first, 16), 16)
                    xh[at, 128 * xx : 128 * xx + 128] = hi
                    xh[at, 512 + 128 * xx : 640 + 128 * xx] = lo

    def arrived(back):
        for n, (g, slab, order) in enumerate(parts):
            wait(g.at[0, 0], rp.at[n, back])

    def split_both(back):
        split(ga, moved(1, (4 - back) % 4)[1], True, 0)
        split(gc, moved(2, (4 - back) % 4)[2], False, 16)

    for n, (g, slab, order) in enumerate(parts):
        plane = box(g, here, order[:2])
        send(plane, plane, sp.at[n], rp.at[n, 0], partner)
    arrived(0)
    split_both(0)
    for back in (1, 3, 2):
        for n, (g, slab, order) in enumerate(parts):
            wait(g.at[0, 0], r3.at[n, back - 1])
            plane = box(g, moved(order[2], 4 - back), order[:2])
            send(plane, plane, sp.at[n], rp.at[n, back], partner)
    for back in (1, 3):
        arrived(back)
        split_both(back)
    arrived(2)

    lane8 = lax.broadcasted_iota(I32, (8, 128), 1)
    zz, yy = here[1], here[2]
    for half in range(2):
        for which in range(2):
            full = None
            for y in range(4):
                tile = gi[zz, yy // 2, 2 * (yy % 2) + half, y]
                turn = (32 * (y - 2 - which)) % 128
                t = tile if turn == 0 else pltpu.roll(tile, turn, 1)
                full = t if full is None else jnp.where(lane8 >= 32 * y, t, full)
            pq[8 * which : 8 * which + 8, 128 * half : 128 * half + 128] = full.astype(I32)

    place = lax.broadcasted_iota(I32, (512, 256), 0)

    def columns(n, carry):
        hot[n] = jnp.where(place == pq[pl.ds(n, 1), :], 1.0, 0.0).astype(BF16)
        return carry

    lax.fori_loop(0, 16, columns, 0)
    split_both(2)
    for n, (g, slab, order) in enumerate(parts):
        wait(g.at[0, 0, 0, 0:3], s1.at[n])
        wait(g.at[0, 0, 0:3], s2.at[n])
        wait(g.at[0:3, 0], s3.at[n])
        wait(g.at[:, 0], sp.at[n])


def table_kernel(gi_ref, xh, hot, out_ref, sm, flat, tx, acc, rows_out, sem):
    r = lax.axis_index("row")
    lane16 = lax.broadcasted_iota(I32, (16, 128), 1)
    by_row = [gi_ref[pl.ds(128 * r + v, 16, stride=8), :] for v in range(8)]
    for u in range(4):
        full = None
        for v in range(8):
            turn = (16 * (v - u)) % 128
            t = by_row[v] if turn == 0 else pltpu.roll(by_row[v], turn, 1)
            full = t if full is None else jnp.where(lane16 >= 16 * v, t, full)
        flat[pl.ds(u, 16, stride=4), :] = full.astype(I32)
    to_scalar = pltpu.make_async_copy(flat, sm, sem.at[0])
    to_scalar.start()

    def tables(nn, *units):
        for extra in range(2):
            n = 2 * nn + extra
            which, l = n // 8, n % 8
            for unit in range(2):
                sums = units[2 * extra + unit]
                rows = pl.ds(pl.multiple_of(512 * which + 256 * unit, 256), 256)
                for half in range(2):
                    pltpu.matmul_push_rhs(hot[n, 256 * half : 256 * half + 256, :], half, unit)
                for half in range(2):
                    pltpu.matmul_acc_lhs(sums, xh[rows, 256 * half : 256 * half + 256], load_staged_rhs=half)
                    pltpu.matmul_acc_lhs(sums, xh[rows, 512 + 256 * half : 768 + 256 * half])
            for unit in range(2):
                t = pltpu.matmul_pop(units[2 * extra + unit])
                tx[pl.ds(8208 * which + 2048 * unit + l, 256, stride=8), :] = t[:, 0:128]
                tx[pl.ds(8208 * which + 4104 + 2048 * unit + l, 256, stride=8), :] = t[:, 128:256]

    def scoped(nn, carry):
        pl.run_scoped(functools.partial(tables, nn), *(pltpu.ACC(unit)((256, 256), F32) for unit in (0, 1, 0, 1)))
        return carry

    lax.fori_loop(0, 8, scoped, 0)
    to_scalar.wait()

    sub = lax.broadcasted_iota(I32, (8, 128), 0)
    low4, low2, low1 = sub < 4, sub % 4 < 2, sub % 2 < 1

    def folded(a):
        b = [
            jnp.where(low4, a[v], a[v + 4]) + pltpu.roll(jnp.where(low4, a[v + 4], a[v]), 4, 0)
            for v in range(4)
        ]
        d = [
            jnp.where(low2, b[v], pltpu.roll(b[v + 2], 2, 0))
            + jnp.where(low2, pltpu.roll(b[v], 6, 0), b[v + 2])
            for v in range(2)
        ]
        return jnp.where(low1, d[0], pltpu.roll(d[1], 1, 0)) + jnp.where(
            low1, pltpu.roll(d[0], 7, 0), d[1]
        )

    def fold_group(n, slot):
        at = pl.ds(pl.multiple_of(8 * n, 8), 8)
        for half in range(2):
            here = [acc[pl.ds(pl.multiple_of(128 * slot + 64 * half + 8 * v, 8), 8), :] for v in range(8)]
            rows_out[at, 128 * half : 128 * half + 128] = folded(here)

    def group(n, carry):
        slot = n % 2
        fold_group(jnp.maximum(n - 1, 0), 1 - slot)
        for v in range(8):
            a0, a1 = None, None
            for k in range(8):
                p = pl.multiple_of(sm[n, 16 * v + k], 8)
                q = pl.multiple_of(sm[n, 16 * v + 8 + k], 8)
                s0 = tx[pl.ds(q, 8), :] * tx[pl.ds(p + 8208, 8), :]
                s1 = tx[pl.ds(q + 4104, 8), :] * tx[pl.ds(p + 12312, 8), :]
                a0 = s0 if a0 is None else a0 + s0
                a1 = s1 if a1 is None else a1 + s1
            acc[pl.ds(pl.multiple_of(128 * slot + 8 * v, 8), 8), :] = a0
            acc[pl.ds(pl.multiple_of(128 * slot + 64 + 8 * v, 8), 8), :] = a1
        return carry

    outs = []
    for part in range(4):
        lax.fori_loop(16 * part, 16 * part + 16, group, 0)
        first, last = max(128 * part - 8, 0), 128 * part + 120
        if part == 3:
            fold_group(63, 1)
            last = 512
        outs.append(
            pltpu.make_async_copy(rows_out.at[first:last], out_ref.at[first:last], sem.at[1 + part])
        )
        outs[-1].start()
    for copy in outs:
        copy.wait()


def gather(x, w, pos, cnt):
    dma = pltpu.SemaphoreType.DMA
    vmem = pltpu.VMEM
    return pl.pallas_call(
        gather_kernel,
        out_shape=(
            jax.ShapeDtypeStruct((4, 2, 4, 4, 8, 128), F32),
            jax.ShapeDtypeStruct((1024, 1152), BF16),
            jax.ShapeDtypeStruct((16, 512, 256), BF16),
        ),
        in_specs=[pl.BlockSpec(memory_space=pltpu.HBM)] * 4,
        out_specs=tuple(pl.BlockSpec(memory_space=vmem) for n in range(3)),
        scratch_shapes=[
            vmem((4, 2, 4, 4, 16, 128), F32),
            vmem((4, 2, 4, 4, 16, 128), F32),
            vmem((31, 62), F32),
            vmem((31, 62), F32),
            vmem((16, 32), I32),
            vmem((32,), I32),
            vmem((16, 128), F32),
            vmem((16, 128), F32),
            vmem((8, 128), F32),
            vmem((16, 256), I32),
            dma((7,)),
            dma((3,)),
            dma((3,)),
            dma((3,)),
            dma((3,)),
            dma((3,)),
            dma((3, 3)),
            dma((3, 3)),
            dma((3, 4)),
        ],
        compiler_params=pltpu.CompilerParams(collective_id=0, has_side_effects=True, vmem_limit_bytes=16 << 20),
        name="gather",
    )(x, w, pos, cnt)


def tabled(gi, xh, hot):
    return pl.pallas_call(
        table_kernel,
        out_shape=jax.ShapeDtypeStruct((512, 256), F32),
        in_specs=[pl.BlockSpec(memory_space=pltpu.VMEM)] * 3,
        out_specs=pl.BlockSpec(memory_space=pl.ANY),
        scratch_shapes=[
            pltpu.SMEM((64, 128), I32),
            pltpu.VMEM((64, 128), I32),
            pltpu.VMEM((16416, 128), F32),
            pltpu.VMEM((256, 128), F32),
            pltpu.VMEM((512, 256), F32),
            pltpu.SemaphoreType.DMA((5,)),
        ],
        compiler_params=pltpu.CompilerParams(vmem_limit_bytes=40 << 20),
        name="tables",
    )(gi, xh, hot)


def shards(moment_x, zinv, positions, entry_count):
    ins = (moment_x.T, zinv.T, positions.T, entry_count)
    gi, xh, hot = gather(*(pltpu.with_memory_space_constraint(a, pltpu.HBM) for a in ins))
    return tabled(gi.reshape(1024, 128), xh, hot)


def solution(mesh):
    return jax.shard_map(
        shards,
        mesh=mesh,
        in_specs=(P("row", "col"), P("row", "col"), P(("row", "col"), None), P(("row", "col"))),
        out_specs=P("row", "col"),
        check_vma=False,
    )
```

time: 41.5 us -> 39.2 us (0.945)
  Pallas kernels: 41.3 us -> 39 us
    pallas_call x1, Pallas kernels: 18.3 us -> 14.7 us  [tabled(): pl.pallas_call(table_kernel, out_shape=jax.ShapeDtypeStruct((512, 256), F...]
    pallas_call x1, Pallas kernels: 23 us -> 24.3 us  [gather(): pl.pallas_call(gather_kernel, out_shape=(jax.ShapeDtypeStruct((4, 2, 4, 4...]
where the time goes in v4:
time: 39.2 us; the launch traced here: 39 us
  Pallas kernels  39 us (99%)
    pallas_call x1, Pallas kernels, gather(): pl.pallas_call(gather_kernel, out_shape=(jax.ShapeDtypeStruct((4, 2, 4, 4...  24.3 us
    pallas_call x1, Pallas kernels, tabled(): pl.pallas_call(table_kernel, out_shape=jax.ShapeDtypeStruct((512, 256), F...  14.7 us

profile of v4, /device:TPU:1, one launch (start us, length us, event | category | flops | bytes accessed | tf_op | source)
XLA Modules:
  0.0 39.0 jit_solution(8315643976635821011)
XLA Ops:
  0.0 24.3 %gather.1 = (f32[4,2,4,4,8,128]{5,4,3,2,1,0:T(8,128)S(1)}, bf16[1024,1152]{1,0:T(8,128)(2,1)S(1)}, bf16[16,512,256]{2,1,0:T(8,128)(2,1)S(1)}) custom-call(f32[31,62]{1,0:T(8,128)} %bitcast.5, f32[31,62]{1,0:T(8,128)} %bitcast.6, s32[16,32]{1,0:T(8,128)} %bitcast.7, s32[32]{0:T(128)} %cnt_in.1), custom_call_target="tpu_custom_call" | custom-call | tf_op jit(solution)/shard_map/gather/pallas_call | solution.py:271
  24.3 14.7 %tables.1 = f32[512,256]{1,0:T(8,128)} custom-call(f32[1024,128]{1,0:T(8,128)S(1)} %bitcast.4, bf16[1024,1152]{1,0:T(8,128)(2,1)S(1)} %get-tuple-element.9.xh, bf16[16,512,256]{2,1,0:T(8,128)(2,1)S(1)} %get-tuple-element.10.hot), custom_call_target="tpu_custom_call" | custom-call | tf_op jit(solution)/shard_map/tables/pallas_call | solution.py:307

commit v5 on v4

--- a/solution.py
+++ b/solution.py
@@ -18,8 +18,8 @@
 
 
 def gather_kernel(
-    x_in, w_in, pos_in, cnt_in, gi, xh, hot,
-    ga, gc, x_ref, w_ref, pos_ref, cnt_ref, slab_a, slab_c, slab_i, pq, loc, s1, s2, s3, sp, r1, r2, r3, rp,
+    x_in, w_in, pos_in, cnt_in, xh, hot, lists, ids, bounds,
+    gi, ga, gc, listed, keys, x_ref, w_ref, pos_ref, cnt_ref, slab_a, slab_c, slab_i, pq, loc, s1, s2, s3, sp, r1, r2, r3, rp,
 ):
     r = lax.axis_index("row")
     c = lax.axis_index("col")
@@ -123,6 +123,59 @@
                     xh[at, 128 * xx : 128 * xx + 128] = hi
                     xh[at, 512 + 128 * xx : 640 + 128 * xx] = lo
 
+    def sort_rows():
+        lane = lax.broadcasted_iota(I32, (8, 128), 1)
+        sub = lax.broadcasted_iota(I32, (8, 128), 0)
+
+        def take(m, carry):
+            tile = gi[here[0], core, m // 4, m % 4]
+            for u in range(4):
+                t = tile if u == 0 else pltpu.roll(tile, 128 - 16 * u, 1)
+                row = 32 * m + 8 * u + sub
+                live = jnp.where((lane >= 8) & (lane < 16) & (t != 248.0), 1.0, 0.0)
+                count = jnp.sum(live, axis=1, keepdims=True)
+                e = t * 0.125
+                h = jnp.floor(e * 0.5)
+                low = pltpu.roll(e - 2.0 * h, 16, 1)
+                value = jnp.where(lane < 16, h, jnp.where(lane < 32, low, 0.0))
+                value = jnp.where(lane == 32, lax.shift_right_logical(row, 1).astype(F32), value)
+                value = jnp.where(lane == 33, (row & 1).astype(F32), value)
+                value = jnp.where(lane == 34, count, value)
+                at = pl.ds(pl.multiple_of(32 * m + 8 * u, 8), 8)
+                listed[at, :] = value
+                keys[at, :] = count * 512.0 + (511 - row).astype(F32)
+            return carry
+
+        lax.fori_loop(0, 16, take, 0)
+        key_row = jnp.transpose(keys[...])[0:1, :]
+
+        def above(b, total):
+            key = keys[pl.ds(pl.multiple_of(8 * b, 8), 8), :]
+            key = jnp.concatenate([key, key, key, key], axis=1)
+            return total + jnp.where(key > key_row, 1.0, 0.0)
+
+        total = lax.fori_loop(0, 64, above, jnp.zeros((8, 512), F32))
+        place = jnp.sum(total, axis=0, keepdims=True).astype(I32)
+        chosen = jnp.where(lax.broadcasted_iota(I32, (512, 512), 0) == place, 1.0, 0.0).astype(BF16)
+        keys[...] = jnp.dot(chosen, listed[...].astype(BF16), preferred_element_type=F32)
+
+        lane64 = lax.broadcasted_iota(I32, (64, 128), 1)
+        flat, names = None, None
+        for v in range(8):
+            t = keys[pl.ds(v, 64, stride=8), :]
+            slots = 16.0 * t + 8.0 * pltpu.roll(t, 112, 1)
+            name = 2.0 * t + pltpu.roll(t, 127, 1)
+            if v == 0:
+                flat = slots
+                names = pltpu.roll(name, 96, 1)
+                reach = jnp.where(t[:, 34:35] >= lane64.astype(F32), 1.0, 0.0)
+                bounds[...] = jnp.broadcast_to(jnp.sum(reach, axis=0, keepdims=True), (8, 128)).astype(I32)
+            else:
+                flat = jnp.where(lane64 >= 16 * v, pltpu.roll(slots, 16 * v, 1), flat)
+                names = jnp.where(lane64 >= v, pltpu.roll(name, 96 + v, 1), names)
+        lists[...] = flat.astype(I32)
+        ids[...] = names.astype(I32)
+
     def arrived(back):
         for n, (g, slab, order) in enumerate(parts):
             wait(g.at[0, 0], rp.at[n, back])
@@ -134,6 +187,7 @@
     for n, (g, slab, order) in enumerate(parts):
         plane = box(g, here, order[:2])
         send(plane, plane, sp.at[n], rp.at[n, 0], partner)
+    sort_rows()
     arrived(0)
     split_both(0)
     for back in (1, 3, 2):
@@ -173,19 +227,13 @@
         wait(g.at[:, 0], sp.at[n])
 
 
-def table_kernel(gi_ref, xh, hot, out_ref, sm, flat, tx, acc, rows_out, sem):
-    r = lax.axis_index("row")
-    lane16 = lax.broadcasted_iota(I32, (16, 128), 1)
-    by_row = [gi_ref[pl.ds(128 * r + v, 16, stride=8), :] for v in range(8)]
-    for u in range(4):
-        full = None
-        for v in range(8):
-            turn = (16 * (v - u)) % 128
-            t = by_row[v] if turn == 0 else pltpu.roll(by_row[v], turn, 1)
-            full = t if full is None else jnp.where(lane16 >= 16 * v, t, full)
-        flat[pl.ds(u, 16, stride=4), :] = full.astype(I32)
-    to_scalar = pltpu.make_async_copy(flat, sm, sem.at[0])
-    to_scalar.start()
+def table_kernel(xh, hot, lists, ids, bounds, out_ref, sm, names, ends, tx, acc, rows_out, sem):
+    to_scalar = [
+        pltpu.make_async_copy(a, b, sem.at[n])
+        for n, (a, b) in enumerate(((lists, sm), (ids, names), (bounds, ends)))
+    ]
+    for copy in to_scalar:
+        copy.start()
 
     def tables(nn, *units):
         for extra in range(2):
@@ -209,7 +257,8 @@
         return carry
 
     lax.fori_loop(0, 8, scoped, 0)
-    to_scalar.wait()
+    for copy in to_scalar:
+        copy.wait()
 
     sub = lax.broadcasted_iota(I32, (8, 128), 0)
     low4, low2, low1 = sub < 4, sub % 4 < 2, sub % 2 < 1
@@ -229,17 +278,18 @@
         )
 
     def fold_group(n, slot):
-        at = pl.ds(pl.multiple_of(8 * n, 8), 8)
         for half in range(2):
             here = [acc[pl.ds(pl.multiple_of(128 * slot + 64 * half + 8 * v, 8), 8), :] for v in range(8)]
-            rows_out[at, 128 * half : 128 * half + 128] = folded(here)
-
-    def group(n, carry):
+            sums = folded(here)
+            for v in range(8):
+                rows_out[pl.ds(512 * half + names[n, v], 1), :] = sums[v : v + 1, :]
+
+    def group(count, n, carry):
         slot = n % 2
         fold_group(jnp.maximum(n - 1, 0), 1 - slot)
         for v in range(8):
             a0, a1 = None, None
-            for k in range(8):
+            for k in range(count):
                 p = pl.multiple_of(sm[n, 16 * v + k], 8)
                 q = pl.multiple_of(sm[n, 16 * v + 8 + k], 8)
                 s0 = tx[pl.ds(q, 8), :] * tx[pl.ds(p + 8208, 8), :]
@@ -250,18 +300,21 @@
             acc[pl.ds(pl.multiple_of(128 * slot + 64 + 8 * v, 8), 8), :] = a1
         return carry
 
-    outs = []
-    for part in range(4):
-        lax.fori_loop(16 * part, 16 * part + 16, group, 0)
-        first, last = max(128 * part - 8, 0), 128 * part + 120
-        if part == 3:
-            fold_group(63, 1)
-            last = 512
-        outs.append(
-            pltpu.make_async_copy(rows_out.at[first:last], out_ref.at[first:last], sem.at[1 + part])
+    first = jnp.int32(0)
+    for count in range(8, 0, -1):
+        last = ends[0, count] if count > 1 else jnp.int32(64)
+        lax.fori_loop(first, last, functools.partial(group, count), 0)
+        first = last
+    fold_group(63, 1)
+    halves = [
+        pltpu.make_async_copy(
+            rows_out.at[512 * half : 512 * half + 512], out_ref.at[:, 128 * half : 128 * half + 128], sem.at[half]
         )
-        outs[-1].start()
-    for copy in outs:
+        for half in range(2)
+    ]
+    for copy in halves:
+        copy.start()
+    for copy in halves:
         copy.wait()
 
 
@@ -271,15 +324,20 @@
     return pl.pallas_call(
         gather_kernel,
         out_shape=(
-            jax.ShapeDtypeStruct((4, 2, 4, 4, 8, 128), F32),
             jax.ShapeDtypeStruct((1024, 1152), BF16),
             jax.ShapeDtypeStruct((16, 512, 256), BF16),
+            jax.ShapeDtypeStruct((64, 128), I32),
+            jax.ShapeDtypeStruct((64, 128), I32),
+            jax.ShapeDtypeStruct((8, 128), I32),
         ),
         in_specs=[pl.BlockSpec(memory_space=pltpu.HBM)] * 4,
-        out_specs=tuple(pl.BlockSpec(memory_space=vmem) for n in range(3)),
+        out_specs=tuple(pl.BlockSpec(memory_space=vmem) for n in range(5)),
         scratch_shapes=[
+            vmem((4, 2, 4, 4, 8, 128), F32),
             vmem((4, 2, 4, 4, 16, 128), F32),
             vmem((4, 2, 4, 4, 16, 128), F32),
+            vmem((512, 128), F32),
+            vmem((512, 128), F32),
             vmem((31, 62), F32),
             vmem((31, 62), F32),
             vmem((16, 32), I32),
@@ -303,29 +361,29 @@
     )(x, w, pos, cnt)
 
 
-def tabled(gi, xh, hot):
+def tabled(*gathered):
     return pl.pallas_call(
         table_kernel,
         out_shape=jax.ShapeDtypeStruct((512, 256), F32),
-        in_specs=[pl.BlockSpec(memory_space=pltpu.VMEM)] * 3,
+        in_specs=[pl.BlockSpec(memory_space=pltpu.VMEM)] * 5,
         out_specs=pl.BlockSpec(memory_space=pl.ANY),
         scratch_shapes=[
             pltpu.SMEM((64, 128), I32),
-            pltpu.VMEM((64, 128), I32),
+            pltpu.SMEM((64, 128), I32),
+            pltpu.SMEM((8, 128), I32),
             pltpu.VMEM((16416, 128), F32),
             pltpu.VMEM((256, 128), F32),
-            pltpu.VMEM((512, 256), F32),
-            pltpu.SemaphoreType.DMA((5,)),
+            pltpu.VMEM((1024, 128), F32),
+            pltpu.SemaphoreType.DMA((3,)),
         ],
         compiler_params=pltpu.CompilerParams(vmem_limit_bytes=40 << 20),
         name="tables",
-    )(gi, xh, hot)
+    )(*gathered)
 
 
 def shards(moment_x, zinv, positions, entry_count):
     ins = (moment_x.T, zinv.T, positions.T, entry_count)
-    gi, xh, hot = gather(*(pltpu.with_memory_space_constraint(a, pltpu.HBM) for a in ins))
-    return tabled(gi.reshape(1024, 128), xh, hot)
+    return tabled(*gather(*(pltpu.with_memory_space_constraint(a, pltpu.HBM) for a in ins)))
 
 
 def solution(mesh):

time: 39.2 us -> 37.9 us (0.967)
  Pallas kernels: 39 us -> 37.8 us
    pallas_call x1, Pallas kernels: 14.7 us -> 12.5 us  [tabled(): pl.pallas_call(table_kernel, out_shape=jax.ShapeDtypeStruct((512, 256), F...]
    pallas_call x1, Pallas kernels: 24.3 us -> 25.3 us  [gather(): pl.pallas_call(gather_kernel, out_shape=(jax.ShapeDtypeStruct((1024, 1152...]
where the time goes in v5:
time: 37.9 us; the launch traced here: 37.8 us
  Pallas kernels  37.8 us (100%)
    pallas_call x1, Pallas kernels, gather(): pl.pallas_call(gather_kernel, out_shape=(jax.ShapeDtypeStruct((1024, 1152...  25.3 us
    pallas_call x1, Pallas kernels, tabled(): pl.pallas_call(table_kernel, out_shape=jax.ShapeDtypeStruct((512, 256), F...  12.5 us

profile of v5, /device:TPU:1, one launch (start us, length us, event | category | flops | bytes accessed | tf_op | source)
XLA Modules:
  0.0 37.8 jit_solution(13887528353897434109)
XLA Ops:
  0.0 25.3 %gather.1 = (bf16[1024,1152]{1,0:T(8,128)(2,1)S(1)}, bf16[16,512,256]{2,1,0:T(8,128)(2,1)S(1)}, s32[64,128]{1,0:T(8,128)S(1)}, s32[64,128]{1,0:T(8,128)S(1)}, s32[8,128]{1,0:T(8,128)S(1)}) custom-call(f32[31,62]{1,0:T(8,128)} %bitcast.3, f32[31,62]{1,0:T(8,128)} %bitcast.4, s32[16,32]{1,0:T(8,128)} %bitcast.5, s32[32]{0:T(128)} %cnt_in.1), custom_call_target="tpu_custom_call" | custom-call | tf_op jit(solution)/shard_map/gather/pallas_call | solution.py:324
  25.3 12.5 %tables.1 = f32[512,256]{1,0:T(8,128)} custom-call(bf16[1024,1152]{1,0:T(8,128)(2,1)S(1)} %get-tuple-element.10.xh, bf16[16,512,256]{2,1,0:T(8,128)(2,1)S(1)} %get-tuple-element.11.hot, s32[64,128]{1,0:T(8,128)S(1)} %get-tuple-element.12.lists, s32[64,128]{1,0:T(8,128)S(1)} %get-tuple-element.13.ids, s32[8,128]{1,0:T(8,128)S(1)} %get-tuple-element.14.bounds), custom_call_target="tpu_custom_call" | custom-call | tf_op jit(solution)/shard_map/tables/pallas_call | solution.py:365

commit v6 on v5

--- a/solution.py
+++ b/solution.py
@@ -176,9 +176,9 @@
         lists[...] = flat.astype(I32)
         ids[...] = names.astype(I32)
 
-    def arrived(back):
-        for n, (g, slab, order) in enumerate(parts):
-            wait(g.at[0, 0], rp.at[n, back])
+    def arrived(back, start):
+        for n in range(start, 3):
+            wait(parts[n][0].at[0, 0], rp.at[n, back])
 
     def split_both(back):
         split(ga, moved(1, (4 - back) % 4)[1], True, 0)
@@ -188,7 +188,7 @@
         plane = box(g, here, order[:2])
         send(plane, plane, sp.at[n], rp.at[n, 0], partner)
     sort_rows()
-    arrived(0)
+    arrived(0, 0)
     split_both(0)
     for back in (1, 3, 2):
         for n, (g, slab, order) in enumerate(parts):
@@ -196,9 +196,10 @@
             plane = box(g, moved(order[2], 4 - back), order[:2])
             send(plane, plane, sp.at[n], rp.at[n, back], partner)
     for back in (1, 3):
-        arrived(back)
+        arrived(back, 1)
         split_both(back)
-    arrived(2)
+    for back in (1, 3, 2):
+        wait(gi.at[0, 0], rp.at[0, back])
 
     lane8 = lax.broadcasted_iota(I32, (8, 128), 1)
     zz, yy = here[1], here[2]
@@ -219,6 +220,7 @@
         return carry
 
     lax.fori_loop(0, 16, columns, 0)
+    arrived(2, 1)
     split_both(2)
     for n, (g, slab, order) in enumerate(parts):
         wait(g.at[0, 0, 0, 0:3], s1.at[n])

time: 37.9 us -> 37.8 us (level)
  no operation moved by 1% of the time
where the time goes in v6:
time: 37.8 us; the launch traced here: 37.6 us
  Pallas kernels  37.6 us (99%)
    pallas_call x1, Pallas kernels, gather(): pl.pallas_call(gather_kernel, out_shape=(jax.ShapeDtypeStruct((1024, 1152...  25.1 us
    pallas_call x1, Pallas kernels, tabled(): pl.pallas_call(table_kernel, out_shape=jax.ShapeDtypeStruct((512, 256), F...  12.5 us

profile of v6, /device:TPU:1, one launch (start us, length us, event | category | flops | bytes accessed | tf_op | source)
XLA Modules:
  0.0 37.6 jit_solution(6300833123857748004)
XLA Ops:
  0.0 25.1 %gather.1 = (bf16[1024,1152]{1,0:T(8,128)(2,1)S(1)}, bf16[16,512,256]{2,1,0:T(8,128)(2,1)S(1)}, s32[64,128]{1,0:T(8,128)S(1)}, s32[64,128]{1,0:T(8,128)S(1)}, s32[8,128]{1,0:T(8,128)S(1)}) custom-call(f32[31,62]{1,0:T(8,128)} %bitcast.3, f32[31,62]{1,0:T(8,128)} %bitcast.4, s32[16,32]{1,0:T(8,128)} %bitcast.5, s32[32]{0:T(128)} %cnt_in.1), custom_call_target="tpu_custom_call" | custom-call | tf_op jit(solution)/shard_map/gather/pallas_call | solution.py:326
  25.1 12.5 %tables.1 = f32[512,256]{1,0:T(8,128)} custom-call(bf16[1024,1152]{1,0:T(8,128)(2,1)S(1)} %get-tuple-element.10.xh, bf16[16,512,256]{2,1,0:T(8,128)(2,1)S(1)} %get-tuple-element.11.hot, s32[64,128]{1,0:T(8,128)S(1)} %get-tuple-element.12.lists, s32[64,128]{1,0:T(8,128)S(1)} %get-tuple-element.13.ids, s32[8,128]{1,0:T(8,128)S(1)} %get-tuple-element.14.bounds), custom_call_target="tpu_custom_call" | custom-call | tf_op jit(solution)/shard_map/tables/pallas_call | solution.py:367

commit v7 on v6

--- a/solution.py
+++ b/solution.py
@@ -19,7 +19,7 @@
 
 def gather_kernel(
     x_in, w_in, pos_in, cnt_in, xh, hot, lists, ids, bounds,
-    gi, ga, gc, listed, keys, x_ref, w_ref, pos_ref, cnt_ref, slab_a, slab_c, slab_i, pq, loc, s1, s2, s3, sp, r1, r2, r3, rp,
+    gi, ga, gc, listed, keys, x_ref, w_ref, pos_ref, cnt_ref, slab_a, slab_c, slab_i, pq, loc, s1, s3, sp, r1, r3, rp,
 ):
     r = lax.axis_index("row")
     c = lax.axis_index("col")
@@ -42,9 +42,20 @@
 
     partner = (r + 1 - 2 * core, c)
     barrier = pltpu.get_barrier_semaphore()
-    for axis in range(3):
-        for offset in (1, 3, 2):
-            pl.semaphore_signal(barrier, inc=1, device_id=device(moved(axis, offset)), device_id_type=MESH)
+    near = [
+        (dx, dz, dy)
+        for dx in range(4)
+        for dz in range(4)
+        for dy in range(4)
+        if dx * dz * dy == 0 and dx + dz + dy > 0
+    ]
+    near.sort(key=lambda o: -sum(min(v, 4 - v) for v in o))
+
+    def shifted(offsets):
+        return [(at + o) % 4 if o else at for at, o in zip(here, offsets)]
+
+    for offsets in near:
+        pl.semaphore_signal(barrier, inc=1, device_id=device(shifted(offsets)), device_id_type=MESH)
     pl.semaphore_signal(barrier, inc=1, device_id=partner, device_id_type=MESH)
 
     for ref in (slab_a, slab_c, slab_i):
@@ -77,7 +88,7 @@
     ]
     for copy in own:
         copy.start()
-    pl.semaphore_wait(barrier, 10)
+    pl.semaphore_wait(barrier, len(near) + 1)
 
     def send(src, dst, send_sem, recv_sem, to):
         pltpu.make_async_remote_copy(
@@ -87,22 +98,19 @@
     def wait(ref, sem):
         pltpu.make_async_copy(ref, ref, sem).wait()
 
-    for n, (g, slab, order) in enumerate(parts):
-        for offset in (1, 3, 2):
-            send(slab, box(g, here), s1.at[n], r1.at[n], device(moved(order[0], offset)))
+    for step in (0, 1, 3, 2):
+        for side in (2, 1, 3, 0):
+            for n, (g, slab, order) in enumerate(parts):
+                if step or side:
+                    offsets = [0, 0, 0]
+                    offsets[order[0]], offsets[order[1]] = step, side
+                    send(slab, box(g, here), s1.at[n, min(step, 1)], r1.at[n, step], device(shifted(offsets)))
     for copy in own:
         copy.wait()
-    for n, (g, slab, order) in enumerate(parts):
-        wait(g.at[0, 0, 0, 0:3], r1.at[n])
-        line = box(g, here, order[:1])
-        for offset in (1, 3, 2):
-            send(line, line, s2.at[n], r2.at[n, offset - 1], device(moved(order[1], offset)))
-        for offset in (1, 3, 2):
-            send(line, line, s3.at[n], r3.at[n, offset - 1], device(moved(order[2], offset)))
-    for back in (1, 3, 2):
+    for back in (0, 1, 3, 2):
         for n, (g, slab, order) in enumerate(parts):
-            wait(g.at[0, 0, 0, 0:4], r2.at[n, back - 1])
-            line = box(g, moved(order[1], 4 - back), order[:1])
+            wait(g.at[0, 0, 0, 0 : 4 if back else 3], r1.at[n, back])
+            line = box(g, moved(order[0], (4 - back) % 4), order[1:2])
             for offset in (1, 3, 2):
                 send(line, line, s3.at[n], r3.at[n, offset - 1], device(moved(order[2], offset)))
     left = lax.broadcasted_iota(I32, (16, 128), 1) < 64
@@ -223,8 +231,8 @@
     arrived(2, 1)
     split_both(2)
     for n, (g, slab, order) in enumerate(parts):
-        wait(g.at[0, 0, 0, 0:3], s1.at[n])
-        wait(g.at[0, 0, 0:3], s2.at[n])
+        wait(g.at[0, 0, 0, 0:3], s1.at[n, 0])
+        wait(g.at[0, 0, 0:3], s1.at[n, 1])
         wait(g.at[0:3, 0], s3.at[n])
         wait(g.at[:, 0], sp.at[n])
 
@@ -349,12 +357,10 @@
             vmem((8, 128), F32),
             vmem((16, 256), I32),
             dma((7,)),
+            dma((3, 2)),
             dma((3,)),
             dma((3,)),
-            dma((3,)),
-            dma((3,)),
-            dma((3,)),
-            dma((3, 3)),
+            dma((3, 4)),
             dma((3, 3)),
             dma((3, 4)),
         ],

time: 37.8 us -> 36 us (0.952)
  Pallas kernels: 37.6 us -> 35.9 us
    pallas_call x1, Pallas kernels: 25.1 us -> 23.4 us  [gather(): pl.pallas_call(gather_kernel, out_shape=(jax.ShapeDtypeStruct((1024, 1152...]
where the time goes in v7:
time: 36 us; the launch traced here: 35.9 us
  Pallas kernels  35.9 us (100%)
    pallas_call x1, Pallas kernels, gather(): pl.pallas_call(gather_kernel, out_shape=(jax.ShapeDtypeStruct((1024, 1152...  23.4 us
    pallas_call x1, Pallas kernels, tabled(): pl.pallas_call(table_kernel, out_shape=jax.ShapeDtypeStruct((512, 256), F...  12.5 us

profile of v7, /device:TPU:1, one launch (start us, length us, event | category | flops | bytes accessed | tf_op | source)
XLA Modules:
  0.0 35.9 jit_solution(13188411257744251446)
XLA Ops:
  0.0 23.4 %gather.1 = (bf16[1024,1152]{1,0:T(8,128)(2,1)S(1)}, bf16[16,512,256]{2,1,0:T(8,128)(2,1)S(1)}, s32[64,128]{1,0:T(8,128)S(1)}, s32[64,128]{1,0:T(8,128)S(1)}, s32[8,128]{1,0:T(8,128)S(1)}) custom-call(f32[31,62]{1,0:T(8,128)} %bitcast.3, f32[31,62]{1,0:T(8,128)} %bitcast.4, s32[16,32]{1,0:T(8,128)} %bitcast.5, s32[32]{0:T(128)} %cnt_in.1), custom_call_target="tpu_custom_call" | custom-call | tf_op jit(solution)/shard_map/gather/pallas_call | solution.py:334
  23.4 12.5 %tables.1 = f32[512,256]{1,0:T(8,128)} custom-call(bf16[1024,1152]{1,0:T(8,128)(2,1)S(1)} %get-tuple-element.10.xh, bf16[16,512,256]{2,1,0:T(8,128)(2,1)S(1)} %get-tuple-element.11.hot, s32[64,128]{1,0:T(8,128)S(1)} %get-tuple-element.12.lists, s32[64,128]{1,0:T(8,128)S(1)} %get-tuple-element.13.ids, s32[8,128]{1,0:T(8,128)S(1)} %get-tuple-element.14.bounds), custom_call_target="tpu_custom_call" | custom-call | tf_op jit(solution)/shard_map/tables/pallas_call | solution.py:373

commit v8 on v7

--- a/solution.py
+++ b/solution.py
@@ -245,28 +245,39 @@
     for copy in to_scalar:
         copy.start()
 
-    def tables(nn, *units):
-        for extra in range(2):
-            n = 2 * nn + extra
-            which, l = n // 8, n % 8
-            for unit in range(2):
-                sums = units[2 * extra + unit]
-                rows = pl.ds(pl.multiple_of(512 * which + 256 * unit, 256), 256)
-                for half in range(2):
-                    pltpu.matmul_push_rhs(hot[n, 256 * half : 256 * half + 256, :], half, unit)
-                for half in range(2):
-                    pltpu.matmul_acc_lhs(sums, xh[rows, 256 * half : 256 * half + 256], load_staged_rhs=half)
-                    pltpu.matmul_acc_lhs(sums, xh[rows, 512 + 256 * half : 768 + 256 * half])
-            for unit in range(2):
-                t = pltpu.matmul_pop(units[2 * extra + unit])
-                tx[pl.ds(8208 * which + 2048 * unit + l, 256, stride=8), :] = t[:, 0:128]
-                tx[pl.ds(8208 * which + 4104 + 2048 * unit + l, 256, stride=8), :] = t[:, 128:256]
-
-    def scoped(nn, carry):
-        pl.run_scoped(functools.partial(tables, nn), *(pltpu.ACC(unit)((256, 256), F32) for unit in (0, 1, 0, 1)))
-        return carry
-
-    lax.fori_loop(0, 8, scoped, 0)
+    def multiply(n, sums):
+        for unit in range(2):
+            rows = pl.ds(pl.multiple_of(512 * (n // 8) + 256 * unit, 256), 256)
+            for half in range(2):
+                pltpu.matmul_push_rhs(hot[n, 256 * half : 256 * half + 256, :], half, unit)
+            for half in range(2):
+                pltpu.matmul_acc_lhs(sums[unit], xh[rows, 256 * half : 256 * half + 256], load_staged_rhs=half)
+                pltpu.matmul_acc_lhs(sums[unit], xh[rows, 512 + 256 * half : 768 + 256 * half])
+
+    def store(n, sums):
+        base = 8208 * (n // 8) + n % 8
+        for unit in range(2):
+            t = pltpu.matmul_pop(sums[unit])
+            tx[pl.ds(base + 2048 * unit, 256, stride=8), :] = t[:, 0:128]
+            tx[pl.ds(base + 4104 + 2048 * unit, 256, stride=8), :] = t[:, 128:256]
+
+    def tables(*units):
+        first, second = units[0:2], units[2:4]
+        multiply(jnp.int32(0), first)
+
+        def pair(nn, carry):
+            multiply(2 * nn + 1, second)
+            store(2 * nn, first)
+            multiply(2 * nn + 2, first)
+            store(2 * nn + 1, second)
+            return carry
+
+        lax.fori_loop(0, 7, pair, 0)
+        multiply(jnp.int32(15), second)
+        store(14, first)
+        store(15, second)
+
+    pl.run_scoped(tables, *(pltpu.ACC(unit)((256, 256), F32) for unit in (0, 1, 0, 1)))
     for copy in to_scalar:
         copy.wait()
 

time: 36 us -> 34.8 us (0.967)
  Pallas kernels: 35.9 us -> 34.7 us
    pallas_call x1, Pallas kernels: 12.5 us -> 11.3 us  [tabled(): pl.pallas_call(table_kernel, out_shape=jax.ShapeDtypeStruct((512, 256), F...]
where the time goes in v8:
time: 34.8 us; the launch traced here: 34.7 us
  Pallas kernels  34.7 us (100%)
    pallas_call x1, Pallas kernels, gather(): pl.pallas_call(gather_kernel, out_shape=(jax.ShapeDtypeStruct((1024, 1152...  23.4 us
    pallas_call x1, Pallas kernels, tabled(): pl.pallas_call(table_kernel, out_shape=jax.ShapeDtypeStruct((512, 256), F...  11.3 us

profile of v8, /device:TPU:1, one launch (start us, length us, event | category | flops | bytes accessed | tf_op | source)
XLA Modules:
  0.0 34.7 jit_solution(5469151820093334829)
XLA Ops:
  0.0 23.4 %gather.1 = (bf16[1024,1152]{1,0:T(8,128)(2,1)S(1)}, bf16[16,512,256]{2,1,0:T(8,128)(2,1)S(1)}, s32[64,128]{1,0:T(8,128)S(1)}, s32[64,128]{1,0:T(8,128)S(1)}, s32[8,128]{1,0:T(8,128)S(1)}) custom-call(f32[31,62]{1,0:T(8,128)} %bitcast.3, f32[31,62]{1,0:T(8,128)} %bitcast.4, s32[16,32]{1,0:T(8,128)} %bitcast.5, s32[32]{0:T(128)} %cnt_in.1), custom_call_target="tpu_custom_call" | custom-call | tf_op jit(solution)/shard_map/gather/pallas_call | solution.py:345
  23.4 11.3 %tables.1 = f32[512,256]{1,0:T(8,128)} custom-call(bf16[1024,1152]{1,0:T(8,128)(2,1)S(1)} %get-tuple-element.10.xh, bf16[16,512,256]{2,1,0:T(8,128)(2,1)S(1)} %get-tuple-element.11.hot, s32[64,128]{1,0:T(8,128)S(1)} %get-tuple-element.12.lists, s32[64,128]{1,0:T(8,128)S(1)} %get-tuple-element.13.ids, s32[8,128]{1,0:T(8,128)S(1)} %get-tuple-element.14.bounds), custom_call_target="tpu_custom_call" | custom-call | tf_op jit(solution)/shard_map/tables/pallas_call | solution.py:384

commit v9 on v8

--- a/solution.py
+++ b/solution.py
@@ -111,7 +111,7 @@
         for n, (g, slab, order) in enumerate(parts):
             wait(g.at[0, 0, 0, 0 : 4 if back else 3], r1.at[n, back])
             line = box(g, moved(order[0], (4 - back) % 4), order[1:2])
-            for offset in (1, 3, 2):
+            for offset in (2, 1, 3):
                 send(line, line, s3.at[n], r3.at[n, offset - 1], device(moved(order[2], offset)))
     left = lax.broadcasted_iota(I32, (16, 128), 1) < 64
 

time: 34.8 us -> 34.9 us (level)
  no operation moved by 1% of the time
where the time goes in v9:
time: 34.9 us; the launch traced here: 34.8 us
  Pallas kernels  34.8 us (100%)
    pallas_call x1, Pallas kernels, gather(): pl.pallas_call(gather_kernel, out_shape=(jax.ShapeDtypeStruct((1024, 1152...  23.5 us
    pallas_call x1, Pallas kernels, tabled(): pl.pallas_call(table_kernel, out_shape=jax.ShapeDtypeStruct((512, 256), F...  11.3 us

profile of v9, /device:TPU:1, one launch (start us, length us, event | category | flops | bytes accessed | tf_op | source)
XLA Modules:
  0.0 34.8 jit_solution(1289536338900970447)
XLA Ops:
  0.0 23.5 %gather.1 = (bf16[1024,1152]{1,0:T(8,128)(2,1)S(1)}, bf16[16,512,256]{2,1,0:T(8,128)(2,1)S(1)}, s32[64,128]{1,0:T(8,128)S(1)}, s32[64,128]{1,0:T(8,128)S(1)}, s32[8,128]{1,0:T(8,128)S(1)}) custom-call(f32[31,62]{1,0:T(8,128)} %bitcast.3, f32[31,62]{1,0:T(8,128)} %bitcast.4, s32[16,32]{1,0:T(8,128)} %bitcast.5, s32[32]{0:T(128)} %cnt_in.1), custom_call_target="tpu_custom_call" | custom-call | tf_op jit(solution)/shard_map/gather/pallas_call | solution.py:345
  23.5 11.3 %tables.1 = f32[512,256]{1,0:T(8,128)} custom-call(bf16[1024,1152]{1,0:T(8,128)(2,1)S(1)} %get-tuple-element.10.xh, bf16[16,512,256]{2,1,0:T(8,128)(2,1)S(1)} %get-tuple-element.11.hot, s32[64,128]{1,0:T(8,128)S(1)} %get-tuple-element.12.lists, s32[64,128]{1,0:T(8,128)S(1)} %get-tuple-element.13.ids, s32[8,128]{1,0:T(8,128)S(1)} %get-tuple-element.14.bounds), custom_call_target="tpu_custom_call" | custom-call | tf_op jit(solution)/shard_map/tables/pallas_call | solution.py:384
